TPU v7x, 256 devices: a whole 4x4x8 slice. The times are simulated.
256 devices in a mesh: snp: 16 (over z, core), trait: 16 (over y, x).
Axes of the slice: x: 4, y: 4, z: 8, core: 2. Of those that a mesh axis runs over, the one named last changes fastest.
Arguments:
- ld_band: float32 [8192, 3072], P('snp'), may hold values from -0.109375 to 0.109375
- marginal: float32 [8192, 4096], P('snp', 'trait'), may hold values from -6 to 6
- effects_init: float32 [8192, 4096], P('snp', 'trait'), may hold values from -6 to 6
- factor_in: float32 [4096, 256], P('trait'), may hold values from -0.09375 to 0.09375
- factor_out: float32 [4096, 256], P('trait'), may hold values from -0.375 to 0.375
- ld_width: int32 [64], replicated, may hold values from 512 to 3072, as said below
- ld_starts: int32 [64], replicated, may hold values from 0 to 8191, as said below
Outputs:
- fitted: float32 [8192, 4096], P('snp', 'trait')
Inputs may be any that keep to these rules, and one draw needn't show every extreme that they name: `ld_width`: every value lies in 512 to 3072; the values 3072 and 512 each occur in every draw. ld_starts[0] is 0, the values rise strictly, and the last one is 8191.
All inputs are finite; a program needn't handle non-finite values.
Results may differ from a plain program's by a relative error of at most 0.0003.
Values sent between devices are 32-bit elements; how exact they have to be, the bound alone decides.
A program may use at most 128 MiB of HBM per device.

v0:
```python
import jax
import jax.numpy as jnp
from jax import lax
from jax.sharding import PartitionSpec as P

STEPS = 2


step_size = 0.5
shrinkage = 0.5


def passed_along(block, axis, distance):
    devices = range(lax.axis_size(axis))
    route = [(i - distance, i) for i in devices if i - distance in devices]
    return lax.ppermute(block, axis, route)


def row_reach(ld_width, ld_starts, row_index, total_rows):
    covered = (ld_starts[None, :] <= row_index[:, None]).astype(jnp.int32)
    following = jnp.concatenate(
        [covered[:, 1:], jnp.zeros((covered.shape[0], 1), jnp.int32)], axis=1
    )
    row_width = jnp.sum((covered - following) * ld_width[None, :], axis=1)
    return jnp.minimum(row_width, total_rows - 1 - row_index)


def shear(ld_rows, reach):
    row_count, band_span = ld_rows.shape
    offsets = lax.broadcasted_iota(jnp.int32, ld_rows.shape, 1)
    masked_band = jnp.where(offsets < reach[:, None], ld_rows, jnp.zeros_like(ld_rows))
    padded = jnp.pad(masked_band, ((0, 0), (0, row_count + 1)))
    full_width = band_span + row_count
    flattened = jnp.concatenate([jnp.zeros((1,), ld_rows.dtype), padded.reshape(-1)])
    return flattened[: row_count * full_width].reshape(row_count, full_width)


def body(ld_band, marginal, effects_init, factor_in, factor_out, ld_width, ld_starts):
    row_count = ld_band.shape[0]
    total_rows = row_count * lax.axis_size("snp")
    hop_count = ld_band.shape[1] // row_count
    local_rows = lax.iota(jnp.int32, row_count)
    row_index = lax.axis_index("snp") * row_count + local_rows
    reach = row_reach(ld_width, ld_starts, row_index, total_rows)
    sheared = shear(ld_band, reach)
    effects = effects_init
    for iteration in range(STEPS):
        ahead = []
        for distance in range(1, hop_count + 1):
            ahead.append(passed_along(effects, "snp", -distance))
        window = jnp.concatenate([effects] + ahead, axis=0)
        upper = jnp.dot(
            sheared, window, precision=lax.Precision.HIGHEST, preferred_element_type=jnp.float32
        )
        transposed = lax.dot_general(
            sheared,
            effects,
            (((0,), (0,)), ((), ())),
            precision=lax.Precision.HIGHEST,
            preferred_element_type=jnp.float32,
        )
        pieces = [
            transposed[tile_index * row_count : (tile_index + 1) * row_count]
            for tile_index in range(hop_count + 1)
        ]
        lower = pieces[0]
        for distance in range(1, hop_count + 1):
            lower = lower + passed_along(pieces[distance], "snp", distance)
        partial_scores = jnp.dot(
            effects, factor_in, precision=lax.Precision.HIGHEST, preferred_element_type=jnp.float32
        )
        scores = lax.psum(partial_scores, "trait")
        projected = lax.dot_general(
            scores,
            factor_out,
            (((1,), (1,)), ((), ())),
            precision=lax.Precision.HIGHEST,
            preferred_element_type=jnp.float32,
        )
        gradient = effects + upper + lower - marginal + shrinkage * (effects - projected)
        effects = effects - step_size * gradient
    return effects


def solution(mesh):
    return jax.shard_map(
        body,
        mesh=mesh,
        in_specs=(
            P("snp", None),
            P("snp", "trait"),
            P("snp", "trait"),
            P("trait", None),
            P("trait", None),
            P(),
            P(),
        ),
        out_specs=P("snp", "trait"),
        check_vma=False,
    )
```

profile of v0, /device:TPU:147, one launch (start us, length us, event | category | flops | bytes accessed | tf_op | source)
XLA Modules:
  0.0 505.4 jit_solution(10433905574596033448)
XLA Ops:
  6.5 2.0 collective-permute-start.5
  8.6 1.9 collective-permute-start.4
  10.5 1.9 collective-permute-start.3
  12.5 1.9 collective-permute-start.1
  14.4 2.7 collective-permute-start
  18.6 3.7 fusion
  22.4 3.6 pad.5
  25.9 11.3 %reshape.18 = f32[1835520]{0:T(1024)} reshape(f32[512,3585]{1,0:T(8,128)} %pad.5) | data formatting | bytes 14684160 | tf_op jit(solution)/shard_map/reshape | solution.py:34
  37.2 6.5 %pad_maximum_fusion = f32[1835008]{0:T(1024)} fusion(f32[1835520]{0:T(1024)} %reshape.18, f32[1]{0:T(128)} %constant.3.clone.1), kind=kLoop, calls=%fused_computation | loop fusion | flops 1835008 | bytes 14682116 | tf_op jit(solution)/shard_map/concatenate | solution.py:34
  43.7 8.4 %reshape.19 = f32[512,3584]{1,0:T(8,128)} reshape(f32[1835008]{0:T(1024)} %pad_maximum_fusion) | data formatting | bytes 14680064 | tf_op jit(solution)/shard_map/reshape | solution.py:35
  52.1 14.6 %fusion.25 = f32[3584,256]{1,0:T(8,128)S(1)} fusion(f32[512,3584]{1,0:T(8,128)} %reshape.19, f32[512,256]{1,0:T(8,128)S(1)} %copy-done.3), kind=kOutput, calls=%fused_computation.51 | convolution fusion | flops 5637144576 | bytes 11534336 | tf_op jit(solution)/shard_map/dot_general | solution.py:55
  66.7 1.9 copy-done.1
  69.9 35.2 %collective-permute-done.1 = f32[512,256]{1,0:T(8,128)S(1)} collective-permute-done((f32[512,256]{1,0:T(8,128)}, f32[512,256]{1,0:T(8,128)S(1)}, u32[]{:S(2)}, u32[]{:S(2)}) %collective-permute-start.1) | collective-permute-done | bytes 524320 | tf_op jit(solution)/shard_map/ppermute | solution.py:16
  105.1 5.4 %collective-permute-start.2 = (f32[512,256]{1,0:T(8,128)S(1)}, f32[512,256]{1,0:T(8,128)}, u32[]{:S(2)}, u32[]{:S(2)}) collective-permute-start(f32[512,256]{1,0:T(8,128)S(1)} %copy-done.3), channel_id=1, source_target_pairs={{48,0},{64,16},{80,32},{96,48},{112,64},{128,80},{144,96},{160,112... | collective-permute-start | bytes 1572872 | tf_op jit(solution)/shard_map/ppermute | solution.py:16
  110.5 2.1 collective-permute-done
  112.6 1.9 collective-permute-start.6
  114.5 1.4 fusion.26
  116.8 1.9 constant_dynamic-update-slice_fusion.5
  118.7 2.0 constant_dynamic-update-slice_fusion.4
  120.7 6.3 %collective-permute-done.2 = f32[512,256]{1,0:T(8,128)} collective-permute-done((f32[512,256]{1,0:T(8,128)S(1)}, f32[512,256]{1,0:T(8,128)}, u32[]{:S(2)}, u32[]{:S(2)}) %collective-permute-start.2) | collective-permute-done | bytes 524320 | tf_op jit(solution)/shard_map/ppermute | solution.py:16
  126.9 1.9 collective-permute-start.11
  128.8 1.9 constant_dynamic-update-slice_fusion.3
  130.7 1.9 collective-permute-start.10
  132.7 1.9 collective-permute-start.9
  134.6 1.9 collective-permute-start.8
  136.5 1.9 collective-permute-start.7
  138.5 1.9 constant_dynamic-update-slice_fusion.2
  140.3 1.9 constant_dynamic-update-slice_fusion.1
  142.2 1.9 constant_dynamic-update-slice_fusion
  144.1 64.9 %all-reduce.5.cloned.1.call-done = f32[512,256]{1,0:T(8,128)} async-done(((f32[512,256]{1,0:T(8,128)}), f32[512,256]{1,0:T(8,128)}) %all-reduce.5.cloned.1.call-update) | async-done | bytes 524304 | tf_op jit(solution)/shard_map/psum | solution.py:72
  209.0 1.8 fusion.2
  210.9 11.0 %collective-permute-done.9 = f32[512,256]{1,0:T(8,128)} collective-permute-done((f32[512,256]{1,0:T(8,128)S(1)}, f32[512,256]{1,0:T(8,128)}, u32[]{:S(2)}, u32[]{:S(2)}) %collective-permute-start.9) | collective-permute-done | bytes 524320 | tf_op jit(solution)/shard_map/ppermute | solution.py:16
  221.9 12.4 %collective-permute-done.8 = f32[512,256]{1,0:T(8,128)} collective-permute-done((f32[512,256]{1,0:T(8,128)S(1)}, f32[512,256]{1,0:T(8,128)}, u32[]{:S(2)}, u32[]{:S(2)}) %collective-permute-start.8) | collective-permute-done | bytes 524320 | tf_op jit(solution)/shard_map/ppermute | solution.py:16
  234.3 11.5 %collective-permute-done.7 = f32[512,256]{1,0:T(8,128)} collective-permute-done((f32[512,256]{1,0:T(8,128)S(1)}, f32[512,256]{1,0:T(8,128)}, u32[]{:S(2)}, u32[]{:S(2)}) %collective-permute-start.7) | collective-permute-done | bytes 524320 | tf_op jit(solution)/shard_map/ppermute | solution.py:16
  245.8 11.2 %constant_dynamic-update-slice_fusion.13 = (f32[3584,256]{1,0:T(8,128)}, f32[512,256]{1,0:T(8,128)S(1)}) fusion(f32[512,256]{1,0:T(8,128)S(1)} %copy-done.3, f32[512,256]{1,0:T(8,128)S(1)} %fusion.2, f32[512,256]{1,0:T(8,128)S(1)} %copy-done.4, f32[512,256]{1,0:T(8,128)} %collective-permute-done.11, f32[512,256]{1,0:T(8,128)} %collective-permute-done.10, ...), kind=kOutput, calls=%fused_computation.46 | convolution fusion | flops 5638717440 | bytes 17301504 | tf_op jit(solution)/shard_map/dot_general | solution.py:52
  257.0 1.9 collective-permute-start.17
  258.9 1.9 collective-permute-start.16
  260.8 2.6 collective-permute-start.14
  263.4 1.9 collective-permute-start.13
  265.4 2.5 collective-permute-start.12
  267.9 12.6 %fusion.27 = f32[3584,256]{1,0:T(8,128)S(1)} fusion(f32[512,3584]{1,0:T(8,128)S(1)} %bitcast.17, f32[512,256]{1,0:T(8,128)S(1)} %get-tuple-element.18), kind=kOutput, calls=%fused_computation.53 | convolution fusion | flops 5637144576 | bytes 11534336 | tf_op jit(solution)/shard_map/dot_general | solution.py:55
  280.4 1.9 copy-done.2
  282.4 1.6 fusion.23
  283.9 63.9 %collective-permute-done.13 = f32[512,256]{1,0:T(8,128)S(1)} collective-permute-done((f32[512,256]{1,0:T(8,128)S(1)}, f32[512,256]{1,0:T(8,128)S(1)}, u32[]{:S(2)}, u32[]{:S(2)}) %collective-permute-start.13) | collective-permute-done | bytes 524320 | tf_op jit(solution)/shard_map/ppermute | solution.py:16
  347.9 2.8 collective-permute-start.15
  350.7 3.6 collective-permute-done.12
  355.1 2.6 collective-permute-start.18
  359.1 1.9 constant_dynamic-update-slice_fusion.12
  361.0 1.9 constant_dynamic-update-slice_fusion.11
  362.9 1.9 collective-permute-start.23
  364.8 1.9 constant_dynamic-update-slice_fusion.10
  366.7 1.9 collective-permute-start.22
  368.6 1.9 collective-permute-start.21
  370.6 2.9 collective-permute-done.15
  373.4 1.9 collective-permute-start.20
  375.4 4.9 collective-permute-start.19
  380.2 1.9 constant_dynamic-update-slice_fusion.9
  382.1 1.9 constant_dynamic-update-slice_fusion.8
  384.0 1.9 constant_dynamic-update-slice_fusion.7
  385.9 75.3 %all-reduce.7.cloned.1.call-done = f32[512,256]{1,0:T(8,128)} async-done(((f32[512,256]{1,0:T(8,128)}), f32[512,256]{1,0:T(8,128)}) %all-reduce.7.cloned.1.call-update) | async-done | bytes 524304 | tf_op jit(solution)/shard_map/psum | solution.py:72
  461.2 1.7 fusion.1
  462.8 7.6 %collective-permute-done.20 = f32[512,256]{1,0:T(8,128)} collective-permute-done((f32[512,256]{1,0:T(8,128)S(1)}, f32[512,256]{1,0:T(8,128)}, u32[]{:S(2)}, u32[]{:S(2)}) %collective-permute-start.20) | collective-permute-done | bytes 524320 | tf_op jit(solution)/shard_map/ppermute | solution.py:16
  470.4 16.8 %collective-permute-done.19 = f32[512,256]{1,0:T(8,128)} collective-permute-done((f32[512,256]{1,0:T(8,128)S(1)}, f32[512,256]{1,0:T(8,128)}, u32[]{:S(2)}, u32[]{:S(2)}) %collective-permute-start.19) | collective-permute-done | bytes 524320 | tf_op jit(solution)/shard_map/ppermute | solution.py:16
  487.2 11.1 %fusion.7 = f32[512,256]{1,0:T(8,128)} fusion(f32[512,256]{1,0:T(8,128)S(1)} %get-tuple-element.18, f32[512,256]{1,0:T(8,128)S(1)} %fusion.1, f32[512,256]{1,0:T(8,128)S(1)} %copy-done.4, f32[512,3584]{1,0:T(8,128)} %reshape.19, f32[3584,256]{1,0:T(8,128)} %constant_dynamic-update-slice_fusion.7, f32[512,256]{1,0:T(8,128)} %collective-permute-done.23, ...), kind=kOutput, calls=%fused_computation.12 | convolution fusion | flops 5638717440 | bytes 16777216 | tf_op jit(solution)/shard_map/dot_general | solution.py:52
  (48 shorter events, 6.0 us)
Async XLA Ops:
  6.5 108.0 %copy-start = (f32[256,256]{1,0:T(8,128)S(1)}, f32[256,256]{1,0:T(8,128)}, u32[]{:S(2)}) copy-start(f32[256,256]{1,0:T(8,128)} %param.10) | copy-start | bytes 786436
  6.5 202.5 %all-reduce.5.cloned.1.call-start = ((), (), s32[]{:S(2)}) async-start(), calls=%async_computation | async-start | bytes 1048576 | tf_op jit(solution)/shard_map/psum | solution.py:72
  6.5 124.2 %collective-permute-start.5 = (f32[512,256]{1,0:T(8,128)}, f32[512,256]{1,0:T(8,128)}, u32[]{:S(2)}, u32[]{:S(2)}) collective-permute-start(f32[512,256]{1,0:T(8,128)} %param.9), channel_id=1, source_target_pairs={{96,0},{112,16},{128,32},{144,48},{160,64},{176,80},{192,96},{208,... | collective-permute-start | bytes 1572872 | tf_op jit(solution)/shard_map/ppermute | solution.py:16
  8.6 124.1 %collective-permute-start.4 = (f32[512,256]{1,0:T(8,128)}, f32[512,256]{1,0:T(8,128)}, u32[]{:S(2)}, u32[]{:S(2)}) collective-permute-start(f32[512,256]{1,0:T(8,128)} %param.9), channel_id=1, source_target_pairs={{80,0},{96,16},{112,32},{128,48},{144,64},{160,80},{176,96},{192,1... | collective-permute-start | bytes 1572872 | tf_op jit(solution)/shard_map/ppermute | solution.py:16
  10.5 124.1 %collective-permute-start.3 = (f32[512,256]{1,0:T(8,128)}, f32[512,256]{1,0:T(8,128)}, u32[]{:S(2)}, u32[]{:S(2)}) collective-permute-start(f32[512,256]{1,0:T(8,128)} %param.9), channel_id=1, source_target_pairs={{64,0},{80,16},{96,32},{112,48},{128,64},{144,80},{160,96},{176,11... | collective-permute-start | bytes 1572872 | tf_op jit(solution)/shard_map/ppermute | solution.py:16
  12.5 92.6 %collective-permute-start.1 = (f32[512,256]{1,0:T(8,128)}, f32[512,256]{1,0:T(8,128)S(1)}, u32[]{:S(2)}, u32[]{:S(2)}) collective-permute-start(f32[512,256]{1,0:T(8,128)} %param.9), channel_id=1, source_target_pairs={{32,0},{48,16},{64,32},{80,48},{96,64},{112,80},{128,96},{144,112}... | collective-permute-start | bytes 1572872 | tf_op jit(solution)/shard_map/ppermute | solution.py:16
  14.4 98.2 %collective-permute-start = (f32[512,256]{1,0:T(8,128)}, f32[512,256]{1,0:T(8,128)}, u32[]{:S(2)}, u32[]{:S(2)}) collective-permute-start(f32[512,256]{1,0:T(8,128)} %param.9), channel_id=1, source_target_pairs={{16,0},{32,16},{48,32},{64,48},{80,64},{96,80},{112,96},{128,112},... | collective-permute-start | bytes 1572872 | tf_op jit(solution)/shard_map/ppermute | solution.py:16
  43.7 8.4 %copy-start.3 = (f32[512,256]{1,0:T(8,128)S(1)}, f32[512,256]{1,0:T(8,128)}, u32[]{:S(2)}) copy-start(f32[512,256]{1,0:T(8,128)} %param.9) | copy-start | bytes 1572868
  66.7 1.9 copy-start.1
  105.1 11.7 %copy-start.7 = (f32[512,256]{1,0:T(8,128)}, f32[512,256]{1,0:T(8,128)S(1)}, u32[]{:S(2)}) copy-start(f32[512,256]{1,0:T(8,128)S(1)} %collective-permute-done.1) | copy-start | bytes 1572868
  105.1 21.8 %collective-permute-start.2 = (f32[512,256]{1,0:T(8,128)S(1)}, f32[512,256]{1,0:T(8,128)}, u32[]{:S(2)}, u32[]{:S(2)}) collective-permute-start(f32[512,256]{1,0:T(8,128)S(1)} %copy-done.3), channel_id=1, source_target_pairs={{48,0},{64,16},{80,32},{96,48},{112,64},{128,80},{144,96},{160,112... | collective-permute-start | bytes 1572872 | tf_op jit(solution)/shard_map/ppermute | solution.py:16
  112.6 23.9 %collective-permute-start.6 = (f32[512,256]{1,0:T(8,128)}, f32[512,256]{1,0:T(8,128)}, u32[]{:S(2)}, u32[]{:S(2)}) collective-permute-start(f32[512,256]{1,0:T(8,128)} %get-tuple-element.11), channel_id=1, source_target_pairs={{0,16},{16,32},{32,48},{48,64},{64,80},{80,96},{96,112},{112,128},... | collective-permute-start | bytes 1572872 | tf_op jit(solution)/shard_map/ppermute | solution.py:16
  115.9 93.1 %copy-start.5 = (f32[256,256]{1,0:T(8,128)S(1)}, f32[256,256]{1,0:T(8,128)}, u32[]{:S(2)}) copy-start(f32[256,256]{1,0:T(8,128)} %param.11) | copy-start | bytes 786436
  115.9 345.2 %all-reduce.7.cloned.1.call-start = ((), (), s32[]{:S(2)}) async-start(), calls=%async_computation.1 | async-start | bytes 1048576 | tf_op jit(solution)/shard_map/psum | solution.py:72
  118.7 127.1 %copy-start.4 = (f32[512,256]{1,0:T(8,128)S(1)}, f32[512,256]{1,0:T(8,128)}, u32[]{:S(2)}) copy-start(f32[512,256]{1,0:T(8,128)} %param.8) | copy-start | bytes 1572868
  126.9 83.9 %collective-permute-start.11 = (f32[512,256]{1,0:T(8,128)}, f32[512,256]{1,0:T(8,128)}, u32[]{:S(2)}, u32[]{:S(2)}) collective-permute-start(f32[512,256]{1,0:T(8,128)} %get-tuple-element.12), channel_id=1, source_target_pairs={{0,96},{16,112},{32,128},{48,144},{64,160},{80,176},{96,192},{112,... | collective-permute-start | bytes 1572872 | tf_op jit(solution)/shard_map/ppermute | solution.py:16
  130.7 80.1 %collective-permute-start.10 = (f32[512,256]{1,0:T(8,128)}, f32[512,256]{1,0:T(8,128)}, u32[]{:S(2)}, u32[]{:S(2)}) collective-permute-start(f32[512,256]{1,0:T(8,128)} %get-tuple-element.13), channel_id=1, source_target_pairs={{0,80},{16,96},{32,112},{48,128},{64,144},{80,160},{96,176},{112,1... | collective-permute-start | bytes 1572872 | tf_op jit(solution)/shard_map/ppermute | solution.py:16
  132.7 89.3 %collective-permute-start.9 = (f32[512,256]{1,0:T(8,128)S(1)}, f32[512,256]{1,0:T(8,128)}, u32[]{:S(2)}, u32[]{:S(2)}) collective-permute-start(f32[512,256]{1,0:T(8,128)S(1)} %get-tuple-element.14), channel_id=1, source_target_pairs={{0,64},{16,80},{32,96},{48,112},{64,128},{80,144},{96,160},{112,17... | collective-permute-start | bytes 1572872 | tf_op jit(solution)/shard_map/ppermute | solution.py:16
  134.6 99.7 %collective-permute-start.8 = (f32[512,256]{1,0:T(8,128)S(1)}, f32[512,256]{1,0:T(8,128)}, u32[]{:S(2)}, u32[]{:S(2)}) collective-permute-start(f32[512,256]{1,0:T(8,128)S(1)} %get-tuple-element.15), channel_id=1, source_target_pairs={{0,48},{16,64},{32,80},{48,96},{64,112},{80,128},{96,144},{112,160... | collective-permute-start | bytes 1572872 | tf_op jit(solution)/shard_map/ppermute | solution.py:16
  136.5 109.3 %collective-permute-start.7 = (f32[512,256]{1,0:T(8,128)S(1)}, f32[512,256]{1,0:T(8,128)}, u32[]{:S(2)}, u32[]{:S(2)}) collective-permute-start(f32[512,256]{1,0:T(8,128)S(1)} %get-tuple-element.16), channel_id=1, source_target_pairs={{0,32},{16,48},{32,64},{48,80},{64,96},{80,112},{96,128},{112,144}... | collective-permute-start | bytes 1572872 | tf_op jit(solution)/shard_map/ppermute | solution.py:16
  209.0 58.8 %slice-start = ((s8[7340032]{0:T(1024)(128)(4,1)}), s8[4194304]{0:T(1024)(128)(4,1)S(1)}, s32[]{:S(2)}) async-start(s8[7340032]{0:T(1024)(128)(4,1)} %bitcast.16), calls=%async_computation.2 | async-start | bytes 8388608
  210.8 57.0 %slice-start.1 = ((s8[7340032]{0:T(1024)(128)(4,1)}), s8[3145728]{0:T(1024)(128)(4,1)S(1)}, s32[]{:S(2)}) async-start(s8[7340032]{0:T(1024)(128)(4,1)} %bitcast.16), calls=%async_computation.3 | async-start | bytes 6291456
  257.0 109.7 %collective-permute-start.17 = (f32[512,256]{1,0:T(8,128)S(1)}, f32[512,256]{1,0:T(8,128)}, u32[]{:S(2)}, u32[]{:S(2)}) collective-permute-start(f32[512,256]{1,0:T(8,128)S(1)} %get-tuple-element.18), channel_id=1, source_target_pairs={{96,0},{112,16},{128,32},{144,48},{160,64},{176,80},{192,96},{208,... | collective-permute-start | bytes 1572872 | tf_op jit(solution)/shard_map/ppermute | solution.py:16
  258.9 109.7 %collective-permute-start.16 = (f32[512,256]{1,0:T(8,128)S(1)}, f32[512,256]{1,0:T(8,128)}, u32[]{:S(2)}, u32[]{:S(2)}) collective-permute-start(f32[512,256]{1,0:T(8,128)S(1)} %get-tuple-element.18), channel_id=1, source_target_pairs={{80,0},{96,16},{112,32},{128,48},{144,64},{160,80},{176,96},{192,1... | collective-permute-start | bytes 1572872 | tf_op jit(solution)/shard_map/ppermute | solution.py:16
  260.8 102.1 %collective-permute-start.14 = (f32[512,256]{1,0:T(8,128)S(1)}, f32[512,256]{1,0:T(8,128)}, u32[]{:S(2)}, u32[]{:S(2)}) collective-permute-start(f32[512,256]{1,0:T(8,128)S(1)} %get-tuple-element.18), channel_id=1, source_target_pairs={{48,0},{64,16},{80,32},{96,48},{112,64},{128,80},{144,96},{160,112... | collective-permute-start | bytes 1572872 | tf_op jit(solution)/shard_map/ppermute | solution.py:16
  263.4 84.4 %collective-permute-start.13 = (f32[512,256]{1,0:T(8,128)S(1)}, f32[512,256]{1,0:T(8,128)S(1)}, u32[]{:S(2)}, u32[]{:S(2)}) collective-permute-start(f32[512,256]{1,0:T(8,128)S(1)} %get-tuple-element.18), channel_id=1, source_target_pairs={{32,0},{48,16},{64,32},{80,48},{96,64},{112,80},{128,96},{144,112}... | collective-permute-start | bytes 1572872 | tf_op jit(solution)/shard_map/ppermute | solution.py:16
  265.4 89.0 %collective-permute-start.12 = (f32[512,256]{1,0:T(8,128)S(1)}, f32[512,256]{1,0:T(8,128)S(1)}, u32[]{:S(2)}, u32[]{:S(2)}) collective-permute-start(f32[512,256]{1,0:T(8,128)S(1)} %get-tuple-element.18), channel_id=1, source_target_pairs={{16,0},{32,16},{48,32},{64,48},{80,64},{96,80},{112,96},{128,112},... | collective-permute-start | bytes 1572872 | tf_op jit(solution)/shard_map/ppermute | solution.py:16
  280.4 1.9 copy-start.2
  347.9 6.5 %copy-start.8 = (f32[512,256]{1,0:T(8,128)}, f32[512,256]{1,0:T(8,128)S(1)}, u32[]{:S(2)}) copy-start(f32[512,256]{1,0:T(8,128)S(1)} %collective-permute-done.13) | copy-start | bytes 1572868
  347.9 25.5 %collective-permute-start.15 = (f32[512,256]{1,0:T(8,128)S(1)}, f32[512,256]{1,0:T(8,128)}, u32[]{:S(2)}, u32[]{:S(2)}) collective-permute-start(f32[512,256]{1,0:T(8,128)S(1)} %get-tuple-element.18), channel_id=1, source_target_pairs={{64,0},{80,16},{96,32},{112,48},{128,64},{144,80},{160,96},{176,11... | collective-permute-start | bytes 1572872 | tf_op jit(solution)/shard_map/ppermute | solution.py:16
  354.3 0.8 copy-start.9
  355.1 20.2 %collective-permute-start.18 = (f32[512,256]{1,0:T(8,128)}, f32[512,256]{1,0:T(8,128)S(1)}, u32[]{:S(2)}, u32[]{:S(2)}) collective-permute-start(f32[512,256]{1,0:T(8,128)} %get-tuple-element.5), channel_id=1, source_target_pairs={{0,16},{16,32},{32,48},{48,64},{64,80},{80,96},{96,112},{112,128},... | collective-permute-start | bytes 1572872 | tf_op jit(solution)/shard_map/ppermute | solution.py:16
  362.9 99.9 %collective-permute-start.23 = (f32[512,256]{1,0:T(8,128)}, f32[512,256]{1,0:T(8,128)}, u32[]{:S(2)}, u32[]{:S(2)}) collective-permute-start(f32[512,256]{1,0:T(8,128)} %get-tuple-element.6), channel_id=1, source_target_pairs={{0,96},{16,112},{32,128},{48,144},{64,160},{80,176},{96,192},{112,... | collective-permute-start | bytes 1572872 | tf_op jit(solution)/shard_map/ppermute | solution.py:16
  366.7 96.1 %collective-permute-start.22 = (f32[512,256]{1,0:T(8,128)}, f32[512,256]{1,0:T(8,128)}, u32[]{:S(2)}, u32[]{:S(2)}) collective-permute-start(f32[512,256]{1,0:T(8,128)} %get-tuple-element.7), channel_id=1, source_target_pairs={{0,80},{16,96},{32,112},{48,128},{64,144},{80,160},{96,176},{112,1... | collective-permute-start | bytes 1572872 | tf_op jit(solution)/shard_map/ppermute | solution.py:16
  368.6 94.2 %collective-permute-start.21 = (f32[512,256]{1,0:T(8,128)}, f32[512,256]{1,0:T(8,128)}, u32[]{:S(2)}, u32[]{:S(2)}) collective-permute-start(f32[512,256]{1,0:T(8,128)} %get-tuple-element.8), channel_id=1, source_target_pairs={{0,64},{16,80},{32,96},{48,112},{64,128},{80,144},{96,160},{112,17... | collective-permute-start | bytes 1572872 | tf_op jit(solution)/shard_map/ppermute | solution.py:16
  373.4 97.0 %collective-permute-start.20 = (f32[512,256]{1,0:T(8,128)S(1)}, f32[512,256]{1,0:T(8,128)}, u32[]{:S(2)}, u32[]{:S(2)}) collective-permute-start(f32[512,256]{1,0:T(8,128)S(1)} %get-tuple-element.9), channel_id=1, source_target_pairs={{0,48},{16,64},{32,80},{48,96},{64,112},{80,128},{96,144},{112,160... | collective-permute-start | bytes 1572872 | tf_op jit(solution)/shard_map/ppermute | solution.py:16
  375.3 10.5 %copy-start.6 = (f32[512,256]{1,0:T(8,128)}, f32[512,256]{1,0:T(8,128)S(1)}, u32[]{:S(2)}) copy-start(f32[512,256]{1,0:T(8,128)S(1)} %collective-permute-done.18) | copy-start | bytes 1572868
  375.4 111.8 %collective-permute-start.19 = (f32[512,256]{1,0:T(8,128)S(1)}, f32[512,256]{1,0:T(8,128)}, u32[]{:S(2)}, u32[]{:S(2)}) collective-permute-start(f32[512,256]{1,0:T(8,128)S(1)} %get-tuple-element.10), channel_id=1, source_target_pairs={{0,32},{16,48},{32,64},{48,80},{64,96},{80,112},{96,128},{112,144}... | collective-permute-start | bytes 1572872 | tf_op jit(solution)/shard_map/ppermute | solution.py:16
Sparse Core Ops, SparseCore 0:
  116.0 92.9 all-reduce.4
  359.2 101.8 all-reduce.6
where the time goes:
time: 513 us; the launch traced here: 505 us
  waiting for transfers between devices  314 us (61%)
  starting transfers between devices  56.2 us (11%)
  matrix products  55.7 us (11%)
  local copies, waits for them, and re-layouts  54.2 us (11%)
  between operations  14.1 us (3%)
  other arithmetic  11.7 us (2%)
    ppermute x24, waiting for transfers between devices, passed_along(): return lax.ppermute(block, axis, route)  173 us
    psum x2, waiting for transfers between devices, body(): scores = lax.psum(partial_scores, 'trait')  140 us
    ppermute x24, starting transfers between devices, passed_along(): return lax.ppermute(block, axis, route)  56.1 us
    dot_general x2, matrix products, body(): lax.dot_general(sheared, effects, (((0,), (0,)), ((), ())), precision=lax...  27.2 us
    unnamed x35, local copies, waits for them, and re-layouts  24.4 us
    dot_general x2, matrix products, body(): jnp.dot(sheared, window, precision=lax.Precision.HIGHEST, preferred_eleme...  22.3 us
    reshape x1, local copies, waits for them, and re-layouts, shear(): padded.reshape(-1)  11.3 us
  transfers between devices with their start and end apart: 26, of which 13 were waited for; matrix products, arithmetic and copies ran while one was open for 19% of the time, Pallas kernels for 0%

commit v1 on v0

v1 whole, which is shorter than its diff:
```python
import jax
import jax.numpy as jnp
from jax import lax
from jax.experimental import pallas as pl
from jax.experimental.pallas import tpu as pltpu
from jax.sharding import PartitionSpec as P

STEPS = 2
MESH = pl.DeviceIdType.MESH
LANES = 128
GROUP = 16

step_size = 0.5
shrinkage = 0.5


def split(values):
    high = values.astype(jnp.bfloat16)
    low = (values - high.astype(jnp.float32)).astype(jnp.bfloat16)
    return high, low


def dot(left, right, contract=((1,), (0,))):
    return lax.dot_general(left, right, (contract, ((), ())), preferred_element_type=jnp.float32)


def kernel(
    total_rows,
    side,
    band_hbm,
    marginal_hbm,
    effects_hbm,
    factor_in_hbm,
    factor_out_hbm,
    width_ref,
    starts_ref,
    out_hbm,
    band,
    reach,
    upper,
    flipped,
    own,
    own_split,
    marginal,
    total,
    ahead,
    beside,
    chain,
    crossed,
    crossing,
    first,
    later,
    factor_in,
    factor_out,
    into_scores,
    from_scores,
    partial,
    from_x,
    over_x,
    from_y,
    over_y,
    scores,
    projected,
    load_sem,
    ahead_send,
    ahead_recv,
    beside_send,
    beside_recv,
    chain_send,
    chain_recv,
    cross_send,
    cross_recv,
    score_send,
    score_recv,
):
    rows = band.shape[0]
    span = band.shape[1]
    hops = span // (2 * rows)
    blocks = 2 * hops + 1
    device = lax.axis_index("snp")
    column = lax.axis_index("trait")
    devices = lax.axis_size("snp")
    core = lax.rem(device, 2)
    behind_id = (lax.rem(device + devices - 2, devices), column)
    ahead_id = (lax.rem(device + 2, devices), column)
    beside_id = (device + 1 - 2 * core, column)
    my_y = lax.div(column, side)
    my_x = lax.rem(column, side)

    def x_peer(offset):
        return lax.rem(my_x + offset, side)

    def y_peer(offset):
        return lax.rem(my_y + offset, side)

    def x_id(offset):
        return (device, my_y * side + x_peer(offset))

    def y_id(offset):
        return (device, y_peer(offset) * side + my_x)

    near = 2 * rows * (hops - 1)
    loads = [
        (effects_hbm.at[:, pl.ds(0, LANES)], own.at[0, 0]),
        (effects_hbm.at[:, pl.ds(LANES, LANES)], own.at[0, 1]),
        (band_hbm.at[:, pl.ds(near, span - near)], band.at[:, pl.ds(near, span - near)]),
        (band_hbm.at[:, pl.ds(0, near)], band.at[:, pl.ds(0, near)]),
        (factor_in_hbm, factor_in),
        (factor_out_hbm, factor_out),
        (marginal_hbm.at[:, pl.ds(0, LANES)], marginal.at[0]),
        (marginal_hbm.at[:, pl.ds(LANES, LANES)], marginal.at[1]),
    ]
    loading = [pltpu.make_async_copy(a, b, load_sem.at[i]) for i, (a, b) in enumerate(loads)]
    for copy in loading:
        copy.start()

    partners = [behind_id, ahead_id, beside_id]
    for offset in range(1, side):
        partners += [x_id(offset), y_id(offset)]
    barrier = pltpu.get_barrier_semaphore()
    for partner in partners:
        pl.semaphore_signal(barrier, inc=1, device_id=partner, device_id_type=MESH)
    pl.semaphore_wait(barrier, len(partners))

    def remote(source, target, send, recv, to):
        return pltpu.make_async_remote_copy(
            src_ref=source, dst_ref=target, send_sem=send, recv_sem=recv, device_id=to, device_id_type=MESH
        )

    def ahead_copy(step, half, slot):
        source = own.at[step, half] if isinstance(slot, int) and slot == 0 else ahead.at[step, half, slot - 1]
        return remote(
            source,
            ahead.at[step, half, slot],
            ahead_send.at[step, half, slot],
            ahead_recv.at[step, half, slot],
            behind_id,
        )

    def beside_copy(source, step, half, slot):
        return remote(
            source,
            beside.at[step, half, slot],
            beside_send.at[step, half, slot],
            beside_recv.at[step, half, slot],
            beside_id,
        )

    def chain_copy(step, half, slot):
        source = first.at[step, half] if slot == 0 else chain.at[step, half, slot - 1]
        return remote(
            source,
            chain.at[step, half, slot],
            chain_send.at[step, half, slot],
            chain_recv.at[step, half, slot],
            ahead_id,
        )

    def cross_copy(step, half, slot):
        return remote(
            crossing.at[step, half, slot],
            crossed.at[step, half, slot],
            cross_send.at[step, half, slot],
            cross_recv.at[step, half, slot],
            beside_id,
        )

    def send_own(step, half):
        ahead_copy(step, half, 0).start()

        @pl.when(core == 1)
        def _():
            beside_copy(own.at[step, half], step, half, 0).start()

    for half in range(2):
        loading[half].wait()
        send_own(0, half)

    def find_reach(group, carry):
        at = pl.multiple_of(group * GROUP, GROUP)
        index = lax.broadcasted_iota(jnp.int32, (GROUP, width_ref.shape[1]), 0) + (device * rows + at)
        entry = lax.broadcasted_iota(jnp.int32, index.shape, 1)
        covered = jnp.where(starts_ref[...] <= index, 1, 0)
        last = jnp.sum(covered, axis=1, keepdims=True) - 1
        width = jnp.sum(jnp.where(entry == last, width_ref[...], 0), axis=1, keepdims=True)
        limit = jnp.minimum(width, total_rows - 1 - index[:, :1])
        reach[pl.ds(at, GROUP), :] = jnp.broadcast_to(limit, (GROUP, LANES))
        return carry

    lax.fori_loop(0, rows // GROUP, find_reach, 0)

    half_rows = rows // 2
    per_block = rows // LANES

    def shear(low_block, high_block):
        for base in range(rows // LANES):
            def body(group, carry):
                shift = group * GROUP
                at = pl.multiple_of(base * LANES + shift, GROUP)
                lane = lax.broadcasted_iota(jnp.int32, (GROUP, LANES), 1)
                row = lax.broadcasted_iota(jnp.int32, (GROUP, LANES), 0)
                row8 = lax.broadcasted_iota(jnp.int32, (8, LANES), 0)
                limit = reach[pl.ds(at, GROUP), :]
                from_left = lane < row + (shift + 1)

                def turned(tile):
                    if tile < 0 or tile >= span // LANES:
                        return jnp.zeros((GROUP, LANES), jnp.float32)
                    values = band[pl.ds(at, GROUP), tile * LANES : (tile + 1) * LANES]
                    values = jnp.where(lane + tile * LANES < limit, values, 0.0)
                    parts = []
                    for top in range(0, GROUP, 8):
                        part = pltpu.roll(values[top : top + 8], shift + (top + 1), 1)
                        for bit in (1, 2, 4):
                            part = jnp.where(row8 & bit != 0, pltpu.roll(part, bit, 1), part)
                        parts.append(part)
                    return jnp.concatenate(parts, axis=0)

                left = turned(low_block * per_block - base - 1)
                for tile in range(low_block * per_block, high_block * per_block):
                    right = turned(tile - base)
                    high, low = split(jnp.where(from_left, left, right))
                    left = right
                    block, at_tile = tile // per_block, tile % per_block
                    row_half = base * LANES // half_rows
                    inner = pl.multiple_of(at - row_half * half_rows, GROUP)
                    lanes = slice(at_tile * LANES, (at_tile + 1) * LANES)
                    upper[block, row_half, 0, pl.ds(inner, GROUP), lanes] = high
                    upper[block, row_half, 1, pl.ds(inner, GROUP), lanes] = low
                return carry

            lax.fori_loop(0, LANES // GROUP, body, 0)

    unit_row = lax.broadcasted_iota(jnp.int32, (half_rows, half_rows), 0)
    unit_column = lax.broadcasted_iota(jnp.int32, (half_rows, half_rows), 1)
    unit = jnp.where(unit_row == unit_column, 1.0, 0.0).astype(jnp.bfloat16)

    def flip(block):
        for part in range(2):
            for i in range(2):
                for j in range(2):
                    tile = upper[block, j, part, :, i * half_rows : (i + 1) * half_rows]
                    turned = dot(unit, tile, ((1,), (1,))).astype(jnp.bfloat16)
                    flipped[block, i, part, :, j * half_rows : (j + 1) * half_rows] = turned

    def product(matrix, block, right, put):
        for i in range(2):
            left = matrix[block, i].reshape(rows, rows)
            found = dot(left, right)
            found = found[:, :LANES] + found[:, LANES:]
            put(i, found[:half_rows] + found[half_rows:])

    def store_to(ref):
        def put(i, values):
            ref[i * half_rows : (i + 1) * half_rows, :] = values

        return put

    def add_to(ref):
        def put(i, values):
            ref[i * half_rows : (i + 1) * half_rows, :] += values

        return put

    def joined(values):
        return jnp.concatenate(split(values), axis=1)

    def start(step, half):
        own_split[half] = joined(own[step, half])
        right = own_split[half]
        product(flipped, 2 * hops - 1, right, store_to(crossing.at[step, half, 0]))
        cross_copy(step, half, 0).start()
        product(flipped, 2 * hops, right, store_to(first.at[step, half]))

        @pl.when(core == 0)
        def _():
            cross_copy(step, half, 0).wait_recv()
            first[step, half] += crossed[step, half, 0]

        chain_copy(step, half, 0).start()

    def finish(step, half):
        last = hops - 1
        ahead_copy(step, half, last).wait_recv()

        @pl.when(core == 0)
        def _():
            beside_copy(ahead.at[step, half, last], step, half, last).start()

        product(upper, 2 * hops, joined(ahead[step, half, last]), add_to(total.at[half]))
        chain_copy(step, half, last).wait_recv()

        @pl.when(core == 1)
        def _():
            cross_copy(step, half, last).wait_recv()
            total[half] += crossed[step, half, last]

        beside_copy(own.at[step, half], step, half, last).wait_recv()
        product(upper, 2 * hops - 1, joined(beside[step, half, last]), add_to(total.at[half]))
        effects = own[step, half]
        gradient = (
            effects
            + (total[half] + chain[step, half, last])
            - marginal[half]
            + shrinkage * (effects - projected[half])
        )
        own[step + 1, half] = effects - step_size * gradient

    def arrive(step, half, slot):
        ahead_copy(step, half, slot).wait_recv()
        ahead_copy(step, half, slot + 1).start()
        beside_copy(ahead.at[step, half, slot], step, half, slot + core).start()
        chain_copy(step, half, slot).wait_recv()
        cross_copy(step, half, slot + 1 - core).wait_recv()
        chain[step, half, slot] += later[half, slot] + crossed[step, half, slot + 1 - core]
        chain_copy(step, half, slot + 1).start()

    def pass_on(step, half, slot):
        right = own_split[half]
        block = 2 * (hops - 1 - slot)
        product(flipped, block - 1, right, store_to(crossing.at[step, half, slot + 1]))
        cross_copy(step, half, slot + 1).start()
        product(flipped, block, right, store_to(later.at[half, slot]))

    def upper_parts(step, half, slot):
        product(upper, 2 * slot + 2, joined(ahead[step, half, slot]), add_to(total.at[half]))
        beside_copy(own.at[step, half], step, half, slot).wait_recv()
        product(upper, 2 * slot + 1, joined(beside[step, half, slot]), add_to(total.at[half]))

    quarter = rows // side
    piece = quarter // side
    x_rows = pl.ds(pl.multiple_of(my_x * quarter, quarter), quarter)
    y_rows = pl.ds(pl.multiple_of(my_y * piece, piece), piece)

    def score_copy(step, phase, offset):
        to_x = pl.ds(pl.multiple_of(x_peer(offset) * quarter, quarter), quarter)
        to_y = pl.ds(pl.multiple_of(y_peer(offset) * piece, piece), piece)
        source, target, to = [
            (partial.at[step, to_x], from_x.at[step, offset - 1], x_id(offset)),
            (over_x.at[step, to_y], from_y.at[step, offset - 1], y_id(offset)),
            (over_y.at[step, y_rows], over_y.at[step, y_rows], y_id(offset)),
            (over_y.at[step], scores.at[step, x_rows], x_id(offset)),
        ][phase]
        return remote(
            source, target, score_send.at[step, phase, offset - 1], score_recv.at[step, phase, offset - 1], to
        )

    def score_recv_wait(step, phase, offset):
        score_copy(step, phase, offset).wait_recv()

    def score_start(step):
        for i in range(2):
            at = slice(i * half_rows, (i + 1) * half_rows)
            found = dot(own_split[0, at], into_scores[0, 0])
            for half, part in ((0, 1), (1, 0), (1, 1)):
                found += dot(own_split[half, at], into_scores[half, part])
            partial[step, at] = found
        for offset in range(1, side):
            score_copy(step, 0, offset).start()

    def score_step(step, phase):
        for offset in range(1, side):
            score_copy(step, phase - 1, offset).wait_recv()
        if phase == 1:
            over_x[step] = partial[step, x_rows] + from_x[step, 0] + from_x[step, 1] + from_x[step, 2]
        if phase == 2:
            over_y[step, y_rows] = over_x[step, y_rows] + from_y[step, 0] + from_y[step, 1] + from_y[step, 2]
        if phase == 3:
            scores[step, x_rows] = over_y[step]
        if phase == 4:
            for i in range(2):
                at = slice(i * half_rows, (i + 1) * half_rows)
                high, low = split(scores[step, at])
                for half in range(2):
                    found = dot(high, from_scores[half], ((1,), (1,)))
                    found += dot(low, from_scores[half], ((1,), (1,)))
                    projected[half, at] = found[:, :LANES] + found[:, LANES:]
            return
        for offset in range(1, side):
            score_copy(step, phase, offset).start()

    loading[2].wait()
    shear(2 * hops - 1, 2 * hops + 1)
    flip(2 * hops - 1)
    flip(2 * hops)

    def prepare():
        loading[4].wait()
        loading[5].wait()
        for half in range(2):
            at = slice(half * LANES, (half + 1) * LANES)
            for part, values in enumerate(split(factor_in[at, :])):
                into_scores[half, part, :LANES] = values
                into_scores[half, part, LANES:] = values
            high, low = split(factor_out[at, :])
            from_scores[half, :LANES] = high
            from_scores[half, LANES:] = low
        loading[3].wait()
        shear(0, 2 * hops - 1)

        def flip_one(block, carry):
            flip(block)
            return carry

        lax.fori_loop(0, 2 * hops - 1, flip_one, 0)
        upper[0] = upper[0] + flipped[0]
        loading[6].wait()
        loading[7].wait()

    def step_body(step, carry):
        def stage(half, carry):
            @pl.when(step > 0)
            def _():
                finish(step - 1, half)

            @pl.when(step == 1)
            def _():
                send_own(step, half)

            @pl.when(step < STEPS)
            def _():
                start(step, half)

            return carry

        lax.fori_loop(0, 2, stage, 0)

        @pl.when(step == 0)
        def _():
            prepare()

        @pl.when(step < STEPS)
        def _():
            def gap(half, carry):
                pass_on(step, half, 0)
                product(upper, 0, own_split[half], store_to(total.at[half]))
                return carry

            lax.fori_loop(0, 2, gap, 0)
            score_start(step)
            for slot in range(hops - 1):
                def event(half, carry):
                    arrive(step, half, slot)
                    if slot + 1 < hops - 1:
                        pass_on(step, half, slot + 1)
                    upper_parts(step, half, slot)
                    for i in range(2):
                        @pl.when(half == i)
                        def _():
                            score_step(step, 2 * slot + i + 1)

                    return carry

                lax.fori_loop(0, 2, event, 0)

        return carry

    lax.fori_loop(0, STEPS + 1, step_body, 0)

    writes = [
        pltpu.make_async_copy(own.at[STEPS, half], out_hbm.at[:, pl.ds(half * LANES, LANES)], load_sem.at[half])
        for half in range(2)
    ]
    for copy in writes:
        copy.start()

    def drain(index, carry):
        step = lax.div(index, 2)
        half = lax.rem(index, 2)
        for slot in range(hops):
            ahead_copy(step, half, slot).wait_send()
            chain_copy(step, half, slot).wait_send()
            cross_copy(step, half, slot).wait_send()
            beside_copy(own.at[step, half], step, half, slot).wait_send()
        return carry

    lax.fori_loop(0, 2 * STEPS, drain, 0)
    for step in range(STEPS):
        for phase in range(4):
            for offset in range(1, side):
                score_copy(step, phase, offset).wait_send()
    for copy in writes:
        copy.wait()


def body(total_rows, side, ld_band, marginal, effects_init, factor_in, factor_out, ld_width, ld_starts):
    rows, span = ld_band.shape
    traits, factors = factor_in.shape
    hops = span // (2 * rows)
    blocks = 2 * hops + 1
    f32, bf16 = jnp.float32, jnp.bfloat16
    piece = (rows, LANES)
    quarter = rows // side
    dma = pltpu.SemaphoreType.DMA
    scratch = [
        pltpu.VMEM((rows, span), f32),
        pltpu.VMEM((rows, LANES), jnp.int32),
        pltpu.VMEM((blocks, 2, 2, rows // 2, rows), bf16),
        pltpu.VMEM((blocks, 2, 2, rows // 2, rows), bf16),
        pltpu.VMEM((STEPS + 1, 2) + piece, f32),
        pltpu.VMEM((2, rows, 2 * LANES), bf16),
        pltpu.VMEM((2,) + piece, f32),
        pltpu.VMEM((2,) + piece, f32),
        pltpu.VMEM((STEPS, 2, hops) + piece, f32),
        pltpu.VMEM((STEPS, 2, hops) + piece, f32),
        pltpu.VMEM((STEPS, 2, hops) + piece, f32),
        pltpu.VMEM((STEPS, 2, hops) + piece, f32),
        pltpu.VMEM((STEPS, 2, hops) + piece, f32),
        pltpu.VMEM((STEPS, 2) + piece, f32),
        pltpu.VMEM((2, hops - 1) + piece, f32),
        pltpu.VMEM((traits, factors), f32),
        pltpu.VMEM((traits, factors), f32),
        pltpu.VMEM((2, 2, 2 * LANES, factors), bf16),
        pltpu.VMEM((2, 2 * LANES, factors), bf16),
        pltpu.VMEM((STEPS, rows, factors), f32),
        pltpu.VMEM((STEPS, side - 1, quarter, factors), f32),
        pltpu.VMEM((STEPS, quarter, factors), f32),
        pltpu.VMEM((STEPS, side - 1, quarter // side, factors), f32),
        pltpu.VMEM((STEPS, quarter, factors), f32),
        pltpu.VMEM((STEPS, rows, factors), f32),
        pltpu.VMEM((2,) + piece, f32),
        dma((8,)),
    ]
    scratch += [dma((STEPS, 2, hops)) for _ in range(8)]
    scratch += [dma((STEPS, 4, side - 1)) for _ in range(2)]

    def call(*refs):
        kernel(total_rows, side, *refs)

    whole = pl.BlockSpec(memory_space=pl.ANY)
    table = pl.BlockSpec(memory_space=pltpu.VMEM)
    return pl.pallas_call(
        call,
        name="fit",
        out_shape=jax.ShapeDtypeStruct(effects_init.shape, f32),
        in_specs=[whole] * 5 + [table] * 2,
        out_specs=whole,
        scratch_shapes=scratch,
        compiler_params=pltpu.CompilerParams(
            collective_id=0, has_side_effects=True, vmem_limit_bytes=60 * 1024 * 1024
        ),
    )(ld_band, marginal, effects_init, factor_in, factor_out, ld_width[None, :], ld_starts[None, :])


def solution(mesh):
    side = 4
    total_rows = mesh.shape["snp"] * 512

    def run(*args):
        return body(total_rows, side, *args)

    return jax.shard_map(
        run,
        mesh=mesh,
        in_specs=(
            P("snp", None),
            P("snp", "trait"),
            P("snp", "trait"),
            P("trait", None),
            P("trait", None),
            P(),
            P(),
        ),
        out_specs=P("snp", "trait"),
        check_vma=False,
    )
```

time: 513 us -> 108 us (0.21)
  the two profiles are of different devices: /device:TPU:147 before, /device:TPU:1 now
where the time goes in v1:
time: 108 us
  Pallas kernels  106 us (98%)
  local copies, waits for them, and re-layouts  1.87 us (2%)
    pallas_call x1, Pallas kernels, body(): pl.pallas_call(call, name='fit', out_shape=jax.ShapeDtypeStruct(effects_i...  106 us

profile of v1, /device:TPU:1, one launch (start us, length us, event | category | flops | bytes accessed | tf_op | source)
XLA Modules:
  0.0 108.3 jit_solution(5124413662134342862)
XLA Ops:
  0.0 106.5 %fit.1 = f32[512,256]{1,0:T(8,128)} custom-call(f32[512,3072]{1,0:T(8,128)} %refs_0_.1, f32[512,256]{1,0:T(8,128)} %refs_1_.1, f32[512,256]{1,0:T(8,128)} %refs_2_.1, f32[256,256]{1,0:T(8,128)} %refs_3_.1, f32[256,256]{1,0:T(8,128)} %refs_4_.1, s32[1,64]{1,0:T(1,128)} %bitcast.2, s32[1,64]{1,0:T(1,128)} %bitcast.3), custom_call_target="tpu_custom_call" | custom-call | tf_op jit(solution)/shard_map/fit/pallas_call | solution.py:532
  106.5 1.9 %copy.9 = f32[512,256]{1,0:T(8,128)} copy(f32[512,256]{1,0:T(8,128)} %fit.1) | data formatting | bytes 1048576

commit v2 on v1

--- a/solution.py
+++ b/solution.py
@@ -38,9 +38,9 @@
     band,
     reach,
     upper,
-    flipped,
     own,
     own_split,
+    own_turned,
     marginal,
     total,
     ahead,
@@ -50,6 +50,7 @@
     crossing,
     first,
     later,
+    home,
     factor_in,
     factor_out,
     into_scores,
@@ -127,8 +128,9 @@
             src_ref=source, dst_ref=target, send_sem=send, recv_sem=recv, device_id=to, device_id_type=MESH
         )
 
-    def ahead_copy(step, half, slot):
-        source = own.at[step, half] if isinstance(slot, int) and slot == 0 else ahead.at[step, half, slot - 1]
+    def ahead_copy(step, half, slot, source=None):
+        if source is None:
+            source = own.at[step, half] if slot == 0 else ahead.at[step, half, slot - 1]
         return remote(
             source,
             ahead.at[step, half, slot],
@@ -173,8 +175,12 @@
             beside_copy(own.at[step, half], step, half, 0).start()
 
     for half in range(2):
-        loading[half].wait()
-        send_own(0, half)
+        source = effects_hbm.at[:, pl.ds(half * LANES, LANES)]
+        ahead_copy(0, half, 0, source).start()
+
+        @pl.when(core == 1)
+        def _():
+            beside_copy(source, 0, half, 0).start()
 
     def find_reach(group, carry):
         at = pl.multiple_of(group * GROUP, GROUP)
@@ -231,22 +237,9 @@
 
             lax.fori_loop(0, LANES // GROUP, body, 0)
 
-    unit_row = lax.broadcasted_iota(jnp.int32, (half_rows, half_rows), 0)
-    unit_column = lax.broadcasted_iota(jnp.int32, (half_rows, half_rows), 1)
-    unit = jnp.where(unit_row == unit_column, 1.0, 0.0).astype(jnp.bfloat16)
-
-    def flip(block):
-        for part in range(2):
-            for i in range(2):
-                for j in range(2):
-                    tile = upper[block, j, part, :, i * half_rows : (i + 1) * half_rows]
-                    turned = dot(unit, tile, ((1,), (1,))).astype(jnp.bfloat16)
-                    flipped[block, i, part, :, j * half_rows : (j + 1) * half_rows] = turned
-
-    def product(matrix, block, right, put):
+    def product(block, right, put):
         for i in range(2):
-            left = matrix[block, i].reshape(rows, rows)
-            found = dot(left, right)
+            found = dot(upper[block, i].reshape(rows, rows), right)
             found = found[:, :LANES] + found[:, LANES:]
             put(i, found[:half_rows] + found[half_rows:])
 
@@ -262,15 +255,30 @@
 
         return put
 
+    def lower_part(block, half, ref):
+        for i in range(2):
+            lanes = slice(i * half_rows, (i + 1) * half_rows)
+            right = upper[block, :, :, :, lanes].reshape(2 * rows, half_rows)
+            found = dot(own_turned[half], right)
+            ref[:, lanes] = found[:LANES] + found[LANES:]
+
     def joined(values):
         return jnp.concatenate(split(values), axis=1)
 
+    def take_own(step, half):
+        values = own[step, half]
+        own_split[half] = joined(values)
+        for part, turned in enumerate(split(values.T)):
+            for i in range(2):
+                piece = turned[:, i * half_rows : (i + 1) * half_rows]
+                for copy in range(2):
+                    at = (2 * i + copy) * half_rows
+                    own_turned[half, part * LANES : (part + 1) * LANES, at : at + half_rows] = piece
+
     def start(step, half):
-        own_split[half] = joined(own[step, half])
-        right = own_split[half]
-        product(flipped, 2 * hops - 1, right, store_to(crossing.at[step, half, 0]))
+        lower_part(2 * hops - 1, half, crossing.at[step, half, 0])
         cross_copy(step, half, 0).start()
-        product(flipped, 2 * hops, right, store_to(first.at[step, half]))
+        lower_part(2 * hops, half, first.at[step, half])
 
         @pl.when(core == 0)
         def _():
@@ -287,23 +295,19 @@
         def _():
             beside_copy(ahead.at[step, half, last], step, half, last).start()
 
-        product(upper, 2 * hops, joined(ahead[step, half, last]), add_to(total.at[half]))
+        product(2 * hops, joined(ahead[step, half, last]), add_to(total.at[half]))
+
+        @pl.when(core == 1)
+        def _():
+            cross_copy(step, half, last).wait_recv()
+            home[half] += crossed[step, half, last]
+
         chain_copy(step, half, last).wait_recv()
-
-        @pl.when(core == 1)
-        def _():
-            cross_copy(step, half, last).wait_recv()
-            total[half] += crossed[step, half, last]
-
+        total[half] += (home[half] + chain[step, half, last]).T
         beside_copy(own.at[step, half], step, half, last).wait_recv()
-        product(upper, 2 * hops - 1, joined(beside[step, half, last]), add_to(total.at[half]))
+        product(2 * hops - 1, joined(beside[step, half, last]), add_to(total.at[half]))
         effects = own[step, half]
-        gradient = (
-            effects
-            + (total[half] + chain[step, half, last])
-            - marginal[half]
-            + shrinkage * (effects - projected[half])
-        )
+        gradient = effects + total[half] - marginal[half] + shrinkage * (effects - projected[half])
         own[step + 1, half] = effects - step_size * gradient
 
     def arrive(step, half, slot):
@@ -312,20 +316,23 @@
         beside_copy(ahead.at[step, half, slot], step, half, slot + core).start()
         chain_copy(step, half, slot).wait_recv()
         cross_copy(step, half, slot + 1 - core).wait_recv()
-        chain[step, half, slot] += later[half, slot] + crossed[step, half, slot + 1 - core]
+        chain[step, half, slot] += later[half] + crossed[step, half, slot + 1 - core]
         chain_copy(step, half, slot + 1).start()
 
     def pass_on(step, half, slot):
-        right = own_split[half]
         block = 2 * (hops - 1 - slot)
-        product(flipped, block - 1, right, store_to(crossing.at[step, half, slot + 1]))
+        lower_part(block - 1, half, crossing.at[step, half, slot + 1])
         cross_copy(step, half, slot + 1).start()
-        product(flipped, block, right, store_to(later.at[half, slot]))
+        lower_part(block, half, later.at[half])
+
+    def diagonal(half):
+        lower_part(0, half, home.at[half])
+        product(0, own_split[half], store_to(total.at[half]))
 
     def upper_parts(step, half, slot):
-        product(upper, 2 * slot + 2, joined(ahead[step, half, slot]), add_to(total.at[half]))
+        product(2 * slot + 2, joined(ahead[step, half, slot]), add_to(total.at[half]))
         beside_copy(own.at[step, half], step, half, slot).wait_recv()
-        product(upper, 2 * slot + 1, joined(beside[step, half, slot]), add_to(total.at[half]))
+        product(2 * slot + 1, joined(beside[step, half, slot]), add_to(total.at[half]))
 
     quarter = rows // side
     piece = quarter // side
@@ -379,90 +386,94 @@
         for offset in range(1, side):
             score_copy(step, phase, offset).start()
 
+    loading[0].wait()
+    loading[1].wait()
+    take_own(0, 0)
     loading[2].wait()
     shear(2 * hops - 1, 2 * hops + 1)
-    flip(2 * hops - 1)
-    flip(2 * hops)
-
-    def prepare():
-        loading[4].wait()
-        loading[5].wait()
+
+    def set_up(step, low, high):
+        @pl.when(step == 0)
+        def _():
+            shear(low, high)
+
+    def step_body(step, carry):
+        @pl.when(step > 0)
+        def _():
+            score_step(step - 1, 4)
+
         for half in range(2):
-            at = slice(half * LANES, (half + 1) * LANES)
-            for part, values in enumerate(split(factor_in[at, :])):
-                into_scores[half, part, :LANES] = values
-                into_scores[half, part, LANES:] = values
-            high, low = split(factor_out[at, :])
-            from_scores[half, :LANES] = high
-            from_scores[half, LANES:] = low
-        loading[3].wait()
-        shear(0, 2 * hops - 1)
-
-        def flip_one(block, carry):
-            flip(block)
-            return carry
-
-        lax.fori_loop(0, 2 * hops - 1, flip_one, 0)
-        upper[0] = upper[0] + flipped[0]
-        loading[6].wait()
-        loading[7].wait()
-
-    def step_body(step, carry):
-        def stage(half, carry):
             @pl.when(step > 0)
             def _():
+                if half == 1:
+                    upper_parts(step - 1, half, 1)
                 finish(step - 1, half)
+
+            @pl.when(step == STEPS)
+            def _():
+                write(half).start()
 
             @pl.when(step == 1)
             def _():
                 send_own(step, half)
+                take_own(step, half)
+
+            if half == 1:
+                @pl.when(step == 0)
+                def _():
+                    take_own(step, half)
 
             @pl.when(step < STEPS)
             def _():
                 start(step, half)
 
-            return carry
-
-        lax.fori_loop(0, 2, stage, 0)
-
         @pl.when(step == 0)
         def _():
-            prepare()
+            loading[3].wait()
+            shear(2 * hops - 3, 2 * hops - 1)
+            loading[4].wait()
+            loading[5].wait()
+            for half in range(2):
+                at = slice(half * LANES, (half + 1) * LANES)
+                for part, values in enumerate(split(factor_in[at, :])):
+                    into_scores[half, part, :LANES] = values
+                    into_scores[half, part, LANES:] = values
+                high, low = split(factor_out[at, :])
+                from_scores[half, :LANES] = high
+                from_scores[half, LANES:] = low
+            loading[6].wait()
+            loading[7].wait()
 
         @pl.when(step < STEPS)
         def _():
-            def gap(half, carry):
-                pass_on(step, half, 0)
-                product(upper, 0, own_split[half], store_to(total.at[half]))
-                return carry
-
-            lax.fori_loop(0, 2, gap, 0)
+            pass_on(step, 0, 0)
             score_start(step)
-            for slot in range(hops - 1):
-                def event(half, carry):
-                    arrive(step, half, slot)
-                    if slot + 1 < hops - 1:
-                        pass_on(step, half, slot + 1)
-                    upper_parts(step, half, slot)
-                    for i in range(2):
-                        @pl.when(half == i)
-                        def _():
-                            score_step(step, 2 * slot + i + 1)
-
-                    return carry
-
-                lax.fori_loop(0, 2, event, 0)
+            arrive(step, 0, 0)
+            pass_on(step, 1, 0)
+            set_up(step, 0, 1)
+            diagonal(0)
+            arrive(step, 1, 0)
+            score_step(step, 1)
+            set_up(step, 1, 3)
+            pass_on(step, 0, 1)
+            diagonal(1)
+            arrive(step, 0, 1)
+            score_step(step, 2)
+            pass_on(step, 1, 1)
+            upper_parts(step, 0, 0)
+            arrive(step, 1, 1)
+            score_step(step, 3)
+            upper_parts(step, 1, 0)
+            upper_parts(step, 0, 1)
 
         return carry
 
+    def write(half):
+        return pltpu.make_async_copy(
+            own.at[STEPS, half], out_hbm.at[:, pl.ds(half * LANES, LANES)], load_sem.at[half]
+        )
+
     lax.fori_loop(0, STEPS + 1, step_body, 0)
-
-    writes = [
-        pltpu.make_async_copy(own.at[STEPS, half], out_hbm.at[:, pl.ds(half * LANES, LANES)], load_sem.at[half])
-        for half in range(2)
-    ]
-    for copy in writes:
-        copy.start()
 
     def drain(index, carry):
         step = lax.div(index, 2)
@@ -479,8 +490,8 @@
         for phase in range(4):
             for offset in range(1, side):
                 score_copy(step, phase, offset).wait_send()
-    for copy in writes:
-        copy.wait()
+    for half in range(2):
+        write(half).wait()
 
 
 def body(total_rows, side, ld_band, marginal, effects_init, factor_in, factor_out, ld_width, ld_starts):
@@ -490,24 +501,26 @@
     blocks = 2 * hops + 1
     f32, bf16 = jnp.float32, jnp.bfloat16
     piece = (rows, LANES)
+    turned = (LANES, rows)
     quarter = rows // side
     dma = pltpu.SemaphoreType.DMA
     scratch = [
         pltpu.VMEM((rows, span), f32),
         pltpu.VMEM((rows, LANES), jnp.int32),
         pltpu.VMEM((blocks, 2, 2, rows // 2, rows), bf16),
-        pltpu.VMEM((blocks, 2, 2, rows // 2, rows), bf16),
         pltpu.VMEM((STEPS + 1, 2) + piece, f32),
         pltpu.VMEM((2, rows, 2 * LANES), bf16),
+        pltpu.VMEM((2, 2 * LANES, 2 * rows), bf16),
         pltpu.VMEM((2,) + piece, f32),
         pltpu.VMEM((2,) + piece, f32),
         pltpu.VMEM((STEPS, 2, hops) + piece, f32),
         pltpu.VMEM((STEPS, 2, hops) + piece, f32),
-        pltpu.VMEM((STEPS, 2, hops) + piece, f32),
-        pltpu.VMEM((STEPS, 2, hops) + piece, f32),
-        pltpu.VMEM((STEPS, 2, hops) + piece, f32),
-        pltpu.VMEM((STEPS, 2) + piece, f32),
-        pltpu.VMEM((2, hops - 1) + piece, f32),
+        pltpu.VMEM((STEPS, 2, hops) + turned, f32),
+        pltpu.VMEM((STEPS, 2, hops) + turned, f32),
+        pltpu.VMEM((STEPS, 2, hops) + turned, f32),
+        pltpu.VMEM((STEPS, 2) + turned, f32),
+        pltpu.VMEM((2,) + turned, f32),
+        pltpu.VMEM((2,) + turned, f32),
         pltpu.VMEM((traits, factors), f32),
         pltpu.VMEM((traits, factors), f32),
         pltpu.VMEM((2, 2, 2 * LANES, factors), bf16),

time: 108 us -> 115 us (1.065)
  Pallas kernels: 106 us -> 113 us
    pallas_call x1, Pallas kernels: 106 us -> 113 us  [body(): pl.pallas_call(call, name='fit', out_shape=jax.ShapeDtypeStruct(effects_i...]
where the time goes in v2:
time: 115 us
  Pallas kernels  113 us (98%)
  local copies, waits for them, and re-layouts  1.87 us (2%)
    pallas_call x1, Pallas kernels, body(): pl.pallas_call(call, name='fit', out_shape=jax.ShapeDtypeStruct(effects_i...  113 us

profile of v2, /device:TPU:1, one launch (start us, length us, event | category | flops | bytes accessed | tf_op | source)
XLA Modules:
  0.0 115.4 jit_solution(16325161050752670096)
XLA Ops:
  0.0 113.5 %fit.1 = f32[512,256]{1,0:T(8,128)} custom-call(f32[512,3072]{1,0:T(8,128)} %refs_0_.1, f32[512,256]{1,0:T(8,128)} %refs_1_.1, f32[512,256]{1,0:T(8,128)} %refs_2_.1, f32[256,256]{1,0:T(8,128)} %refs_3_.1, f32[256,256]{1,0:T(8,128)} %refs_4_.1, s32[1,64]{1,0:T(1,128)} %bitcast.2, s32[1,64]{1,0:T(1,128)} %bitcast.3), custom_call_target="tpu_custom_call" | custom-call | tf_op jit(solution)/shard_map/fit/pallas_call | solution.py:545
  113.5 1.9 %copy.9 = f32[512,256]{1,0:T(8,128)} copy(f32[512,256]{1,0:T(8,128)} %fit.1) | data formatting | bytes 1048576

commit v3 on v2

--- a/solution.py
+++ b/solution.py
@@ -32,15 +32,17 @@
     effects_hbm,
     factor_in_hbm,
     factor_out_hbm,
-    width_ref,
-    starts_ref,
+    width_hbm,
+    starts_hbm,
     out_hbm,
+    width,
+    starts,
     band,
     reach,
     upper,
     own,
     own_split,
-    own_turned,
+    own_stack,
     marginal,
     total,
     ahead,
@@ -102,6 +104,8 @@
 
     near = 2 * rows * (hops - 1)
     loads = [
+        (width_hbm, width),
+        (starts_hbm, starts),
         (effects_hbm.at[:, pl.ds(0, LANES)], own.at[0, 0]),
         (effects_hbm.at[:, pl.ds(LANES, LANES)], own.at[0, 1]),
         (band_hbm.at[:, pl.ds(near, span - near)], band.at[:, pl.ds(near, span - near)]),
@@ -182,32 +186,29 @@
         def _():
             beside_copy(source, 0, half, 0).start()
 
-    def find_reach(group, carry):
-        at = pl.multiple_of(group * GROUP, GROUP)
-        index = lax.broadcasted_iota(jnp.int32, (GROUP, width_ref.shape[1]), 0) + (device * rows + at)
-        entry = lax.broadcasted_iota(jnp.int32, index.shape, 1)
-        covered = jnp.where(starts_ref[...] <= index, 1, 0)
-        last = jnp.sum(covered, axis=1, keepdims=True) - 1
-        width = jnp.sum(jnp.where(entry == last, width_ref[...], 0), axis=1, keepdims=True)
-        limit = jnp.minimum(width, total_rows - 1 - index[:, :1])
-        reach[pl.ds(at, GROUP), :] = jnp.broadcast_to(limit, (GROUP, LANES))
-        return carry
-
-    lax.fori_loop(0, rows // GROUP, find_reach, 0)
+    def find_reach():
+        for base in range(0, rows, LANES):
+            index = lax.broadcasted_iota(jnp.int32, (LANES, width.shape[1]), 0) + (device * rows + base)
+            entry = lax.broadcasted_iota(jnp.int32, index.shape, 1)
+            covered = jnp.where(starts[...] <= index, 1, 0)
+            last = jnp.sum(covered, axis=1, keepdims=True) - 1
+            found = jnp.sum(jnp.where(entry == last, width[...], 0), axis=1, keepdims=True)
+            limit = jnp.minimum(found, total_rows - 1 - index[:, :1])
+            reach[base : base + LANES, :] = jnp.broadcast_to(limit, (LANES, LANES))
 
     half_rows = rows // 2
     per_block = rows // LANES
 
     def shear(low_block, high_block):
-        for base in range(rows // LANES):
-            def body(group, carry):
-                shift = group * GROUP
+        def body(group, carry):
+            shift = group * GROUP
+            lane = lax.broadcasted_iota(jnp.int32, (GROUP, LANES), 1)
+            row = lax.broadcasted_iota(jnp.int32, (GROUP, LANES), 0)
+            row8 = lax.broadcasted_iota(jnp.int32, (8, LANES), 0)
+            from_left = lane < row + (shift + 1)
+            for base in range(rows // LANES):
                 at = pl.multiple_of(base * LANES + shift, GROUP)
-                lane = lax.broadcasted_iota(jnp.int32, (GROUP, LANES), 1)
-                row = lax.broadcasted_iota(jnp.int32, (GROUP, LANES), 0)
-                row8 = lax.broadcasted_iota(jnp.int32, (8, LANES), 0)
                 limit = reach[pl.ds(at, GROUP), :]
-                from_left = lane < row + (shift + 1)
 
                 def turned(tile):
                     if tile < 0 or tile >= span // LANES:
@@ -233,9 +234,9 @@
                     lanes = slice(at_tile * LANES, (at_tile + 1) * LANES)
                     upper[block, row_half, 0, pl.ds(inner, GROUP), lanes] = high
                     upper[block, row_half, 1, pl.ds(inner, GROUP), lanes] = low
-                return carry
-
-            lax.fori_loop(0, LANES // GROUP, body, 0)
+            return carry
+
+        lax.fori_loop(0, LANES // GROUP, body, 0)
 
     def product(block, right, put):
         for i in range(2):
@@ -258,22 +259,20 @@
     def lower_part(block, half, ref):
         for i in range(2):
             lanes = slice(i * half_rows, (i + 1) * half_rows)
-            right = upper[block, :, :, :, lanes].reshape(2 * rows, half_rows)
-            found = dot(own_turned[half], right)
-            ref[:, lanes] = found[:LANES] + found[LANES:]
+            left = upper[block, :, :, :, lanes].reshape(2 * rows, half_rows)
+            found = dot(left, own_stack[half], ((0,), (0,)))
+            ref[lanes, :] = found[:, :LANES] + found[:, LANES:]
 
     def joined(values):
         return jnp.concatenate(split(values), axis=1)
 
     def take_own(step, half):
-        values = own[step, half]
-        own_split[half] = joined(values)
-        for part, turned in enumerate(split(values.T)):
-            for i in range(2):
-                piece = turned[:, i * half_rows : (i + 1) * half_rows]
-                for copy in range(2):
-                    at = (2 * i + copy) * half_rows
-                    own_turned[half, part * LANES : (part + 1) * LANES, at : at + half_rows] = piece
+        found = joined(own[step, half])
+        own_split[half] = found
+        for i in range(2):
+            for copy in range(2):
+                at = (2 * i + copy) * half_rows
+                own_stack[half, at : at + half_rows] = found[i * half_rows : (i + 1) * half_rows]
 
     def start(step, half):
         lower_part(2 * hops - 1, half, crossing.at[step, half, 0])
@@ -302,21 +301,24 @@
             cross_copy(step, half, last).wait_recv()
             home[half] += crossed[step, half, last]
 
-        chain_copy(step, half, last).wait_recv()
-        total[half] += (home[half] + chain[step, half, last]).T
         beside_copy(own.at[step, half], step, half, last).wait_recv()
         product(2 * hops - 1, joined(beside[step, half, last]), add_to(total.at[half]))
+        chain_copy(step, half, last).wait_recv()
         effects = own[step, half]
-        gradient = effects + total[half] - marginal[half] + shrinkage * (effects - projected[half])
+        product_sum = total[half] + (home[half] + chain[step, half, last])
+        gradient = effects + product_sum - marginal[half] + shrinkage * (effects - projected[half])
         own[step + 1, half] = effects - step_size * gradient
 
-    def arrive(step, half, slot):
+    def arrive_ahead(step, half, slot):
         ahead_copy(step, half, slot).wait_recv()
         ahead_copy(step, half, slot + 1).start()
         beside_copy(ahead.at[step, half, slot], step, half, slot + core).start()
+
+    def arrive_chain(step, half, slot):
+        cross_copy(step, half, slot + 1 - core).wait_recv()
+        later[half] += crossed[step, half, slot + 1 - core]
         chain_copy(step, half, slot).wait_recv()
-        cross_copy(step, half, slot + 1 - core).wait_recv()
-        chain[step, half, slot] += later[half] + crossed[step, half, slot + 1 - core]
+        chain[step, half, slot] += later[half]
         chain_copy(step, half, slot + 1).start()
 
     def pass_on(step, half, slot):
@@ -388,51 +390,31 @@
 
     loading[0].wait()
     loading[1].wait()
+    find_reach()
+    loading[2].wait()
+    loading[3].wait()
     take_own(0, 0)
-    loading[2].wait()
+    loading[4].wait()
     shear(2 * hops - 1, 2 * hops + 1)
 
     def set_up(step, low, high):
         @pl.when(step == 0)
         def _():
-            shear(low, high)
-
-    def step_body(step, carry):
-        @pl.when(step > 0)
-        def _():
-            score_step(step - 1, 4)
-
-        for half in range(2):
-            @pl.when(step > 0)
-            def _():
-                if half == 1:
-                    upper_parts(step - 1, half, 1)
-                finish(step - 1, half)
-
-            @pl.when(step == STEPS)
-            def _():
-                write(half).start()
-
-            @pl.when(step == 1)
-            def _():
-                send_own(step, half)
-                take_own(step, half)
-
-            if half == 1:
-                @pl.when(step == 0)
-                def _():
-                    take_own(step, half)
-
-            @pl.when(step < STEPS)
-            def _():
-                start(step, half)
-
+            for block in range(high - 1, low - 1, -1):
+                shear(block, block + 1)
+
+    def set_up_far(step):
         @pl.when(step == 0)
         def _():
-            loading[3].wait()
-            shear(2 * hops - 3, 2 * hops - 1)
-            loading[4].wait()
             loading[5].wait()
+            shear(2 * hops - 2, 2 * hops - 1)
+            shear(2 * hops - 3, 2 * hops - 2)
+
+    def set_up_factors(step):
+        @pl.when(step == 0)
+        def _():
+            loading[6].wait()
+            loading[7].wait()
             for half in range(2):
                 at = slice(half * LANES, (half + 1) * LANES)
                 for part, values in enumerate(split(factor_in[at, :])):
@@ -441,29 +423,65 @@
                 high, low = split(factor_out[at, :])
                 from_scores[half, :LANES] = high
                 from_scores[half, LANES:] = low
-            loading[6].wait()
-            loading[7].wait()
+            loading[8].wait()
+            loading[9].wait()
+
+    def step_body(step, carry):
+        @pl.when(step > 0)
+        def _():
+            score_step(step - 1, 4)
+
+        for half in range(2):
+            @pl.when(step > 0)
+            def _():
+                if half == 1:
+                    upper_parts(step - 1, half, 1)
+                finish(step - 1, half)
+
+            @pl.when(step == STEPS)
+            def _():
+                write(half).start()
+
+            @pl.when(step == 1)
+            def _():
+                send_own(step, half)
+                take_own(step, half)
+
+            if half == 1:
+                @pl.when(step == 0)
+                def _():
+                    take_own(step, half)
+
+            @pl.when(step < STEPS)
+            def _():
+                start(step, half)
 
         @pl.when(step < STEPS)
         def _():
+            arrive_ahead(step, 0, 0)
+            set_up_far(step)
             pass_on(step, 0, 0)
+            arrive_chain(step, 0, 0)
+            arrive_ahead(step, 1, 0)
+            pass_on(step, 1, 0)
+            set_up_factors(step)
             score_start(step)
-            arrive(step, 0, 0)
-            pass_on(step, 1, 0)
+            arrive_chain(step, 1, 0)
+            set_up(step, 1, 3)
+            arrive_ahead(step, 0, 1)
+            pass_on(step, 0, 1)
+            arrive_chain(step, 0, 1)
+            score_step(step, 1)
+            arrive_ahead(step, 1, 1)
+            pass_on(step, 1, 1)
             set_up(step, 0, 1)
             diagonal(0)
-            arrive(step, 1, 0)
-            score_step(step, 1)
-            set_up(step, 1, 3)
-            pass_on(step, 0, 1)
+            arrive_chain(step, 1, 1)
+            score_step(step, 2)
             diagonal(1)
-            arrive(step, 0, 1)
-            score_step(step, 2)
-            pass_on(step, 1, 1)
             upper_parts(step, 0, 0)
-            arrive(step, 1, 1)
+            upper_parts(step, 1, 0)
             score_step(step, 3)
-            upper_parts(step, 1, 0)
             upper_parts(step, 0, 1)
 
         return carry
@@ -501,26 +519,27 @@
     blocks = 2 * hops + 1
     f32, bf16 = jnp.float32, jnp.bfloat16
     piece = (rows, LANES)
-    turned = (LANES, rows)
     quarter = rows // side
     dma = pltpu.SemaphoreType.DMA
     scratch = [
+        pltpu.VMEM((1,) + ld_width.shape, jnp.int32),
+        pltpu.VMEM((1,) + ld_starts.shape, jnp.int32),
         pltpu.VMEM((rows, span), f32),
         pltpu.VMEM((rows, LANES), jnp.int32),
         pltpu.VMEM((blocks, 2, 2, rows // 2, rows), bf16),
         pltpu.VMEM((STEPS + 1, 2) + piece, f32),
         pltpu.VMEM((2, rows, 2 * LANES), bf16),
-        pltpu.VMEM((2, 2 * LANES, 2 * rows), bf16),
+        pltpu.VMEM((2, 2 * rows, 2 * LANES), bf16),
         pltpu.VMEM((2,) + piece, f32),
         pltpu.VMEM((2,) + piece, f32),
         pltpu.VMEM((STEPS, 2, hops) + piece, f32),
         pltpu.VMEM((STEPS, 2, hops) + piece, f32),
-        pltpu.VMEM((STEPS, 2, hops) + turned, f32),
-        pltpu.VMEM((STEPS, 2, hops) + turned, f32),
-        pltpu.VMEM((STEPS, 2, hops) + turned, f32),
-        pltpu.VMEM((STEPS, 2) + turned, f32),
-        pltpu.VMEM((2,) + turned, f32),
-        pltpu.VMEM((2,) + turned, f32),
+        pltpu.VMEM((STEPS, 2, hops) + piece, f32),
+        pltpu.VMEM((STEPS, 2, hops) + piece, f32),
+        pltpu.VMEM((STEPS, 2, hops) + piece, f32),
+        pltpu.VMEM((STEPS, 2) + piece, f32),
+        pltpu.VMEM((2,) + piece, f32),
+        pltpu.VMEM((2,) + piece, f32),
         pltpu.VMEM((traits, factors), f32),
         pltpu.VMEM((traits, factors), f32),
         pltpu.VMEM((2, 2, 2 * LANES, factors), bf16),
@@ -532,7 +551,7 @@
         pltpu.VMEM((STEPS, quarter, factors), f32),
         pltpu.VMEM((STEPS, rows, factors), f32),
         pltpu.VMEM((2,) + piece, f32),
-        dma((8,)),
+        dma((10,)),
     ]
     scratch += [dma((STEPS, 2, hops)) for _ in range(8)]
     scratch += [dma((STEPS, 4, side - 1)) for _ in range(2)]
@@ -541,12 +560,11 @@
         kernel(total_rows, side, *refs)
 
     whole = pl.BlockSpec(memory_space=pl.ANY)
-    table = pl.BlockSpec(memory_space=pltpu.VMEM)
     return pl.pallas_call(
         call,
         name="fit",
         out_shape=jax.ShapeDtypeStruct(effects_init.shape, f32),
-        in_specs=[whole] * 5 + [table] * 2,
+        in_specs=[whole] * 7,
         out_specs=whole,
         scratch_shapes=scratch,
         compiler_params=pltpu.CompilerParams(

time: 115 us -> 98.7 us (0.86)
  Pallas kernels: 113 us -> 96.7 us
    pallas_call x1, Pallas kernels: 113 us -> 96.7 us  [body(): pl.pallas_call(call, name='fit', out_shape=jax.ShapeDtypeStruct(effects_i...]
where the time goes in v3:
time: 98.7 us; the launch traced here: 98.6 us
  Pallas kernels  96.7 us (98%)
  local copies, waits for them, and re-layouts  1.87 us (2%)
    pallas_call x1, Pallas kernels, body(): pl.pallas_call(call, name='fit', out_shape=jax.ShapeDtypeStruct(effects_i...  96.7 us

profile of v3, /device:TPU:1, one launch (start us, length us, event | category | flops | bytes accessed | tf_op | source)
XLA Modules:
  0.0 98.6 jit_solution(13439680198509157895)
XLA Ops:
  0.0 96.7 %fit.1 = f32[512,256]{1,0:T(8,128)} custom-call(f32[512,3072]{1,0:T(8,128)} %refs_0_.1, f32[512,256]{1,0:T(8,128)} %refs_1_.1, f32[512,256]{1,0:T(8,128)} %refs_2_.1, f32[256,256]{1,0:T(8,128)} %refs_3_.1, f32[256,256]{1,0:T(8,128)} %refs_4_.1, s32[1,64]{1,0:T(1,128)} %bitcast.2, s32[1,64]{1,0:T(1,128)} %bitcast.3), custom_call_target="tpu_custom_call" | custom-call | tf_op jit(solution)/shard_map/fit/pallas_call | solution.py:563
  96.7 1.9 %copy.9 = f32[512,256]{1,0:T(8,128)} copy(f32[512,256]{1,0:T(8,128)} %fit.1) | data formatting | bytes 1048576

commit v4 on v3

--- a/solution.py
+++ b/solution.py
@@ -58,10 +58,10 @@
     into_scores,
     from_scores,
     partial,
-    from_x,
-    over_x,
-    from_y,
-    over_y,
+    from_along,
+    over_along,
+    from_across,
+    over_both,
     scores,
     projected,
     load_sem,
@@ -286,7 +286,7 @@
 
         chain_copy(step, half, 0).start()
 
-    def finish(step, half):
+    def finish_ahead(step, half):
         last = hops - 1
         ahead_copy(step, half, last).wait_recv()
 
@@ -303,6 +303,9 @@
 
         beside_copy(own.at[step, half], step, half, last).wait_recv()
         product(2 * hops - 1, joined(beside[step, half, last]), add_to(total.at[half]))
+
+    def finish_chain(step, half):
+        last = hops - 1
         chain_copy(step, half, last).wait_recv()
         effects = own[step, half]
         product_sum = total[half] + (home[half] + chain[step, half, last])
@@ -336,26 +339,54 @@
         beside_copy(own.at[step, half], step, half, slot).wait_recv()
         product(2 * slot + 1, joined(beside[step, half, slot]), add_to(total.at[half]))
 
-    quarter = rows // side
+    quarter = half_rows // side
     piece = quarter // side
-    x_rows = pl.ds(pl.multiple_of(my_x * quarter, quarter), quarter)
-    y_rows = pl.ds(pl.multiple_of(my_y * piece, piece), piece)
-
-    def score_copy(step, phase, offset):
-        to_x = pl.ds(pl.multiple_of(x_peer(offset) * quarter, quarter), quarter)
-        to_y = pl.ds(pl.multiple_of(y_peer(offset) * piece, piece), piece)
+    places = (my_x, my_y)
+    peers = (x_peer, y_peer)
+    ids = (x_id, y_id)
+
+    def stripe(group, index):
+        return pl.ds(pl.multiple_of(group * half_rows + index * quarter, quarter), quarter)
+
+    def strip(index):
+        return pl.ds(pl.multiple_of(index * piece, piece), piece)
+
+    def score_copy(step, group, phase, offset):
+        along, across = group, 1 - group
         source, target, to = [
-            (partial.at[step, to_x], from_x.at[step, offset - 1], x_id(offset)),
-            (over_x.at[step, to_y], from_y.at[step, offset - 1], y_id(offset)),
-            (over_y.at[step, y_rows], over_y.at[step, y_rows], y_id(offset)),
-            (over_y.at[step], scores.at[step, x_rows], x_id(offset)),
+            (
+                partial.at[step, stripe(group, peers[along](offset))],
+                from_along.at[step, group, offset - 1],
+                ids[along](offset),
+            ),
+            (
+                over_along.at[step, group, strip(peers[across](offset))],
+                from_across.at[step, group, offset - 1],
+                ids[across](offset),
+            ),
+            (
+                over_both.at[step, group, strip(places[across])],
+                over_both.at[step, group, strip(places[across])],
+                ids[across](offset),
+            ),
+            (
+                over_both.at[step, group],
+                scores.at[step, stripe(group, places[along])],
+                ids[along](offset),
+            ),
         ][phase]
         return remote(
-            source, target, score_send.at[step, phase, offset - 1], score_recv.at[step, phase, offset - 1], to
+            source,
+            target,
+            score_send.at[step, group, phase, offset - 1],
+            score_recv.at[step, group, phase, offset - 1],
+            to,
         )
 
-    def score_recv_wait(step, phase, offset):
-        score_copy(step, phase, offset).wait_recv()
+    def score_send_all(step, phase):
+        for offset in range(1, side):
+            for group in range(2):
+                score_copy(step, group, phase, offset).start()
 
     def score_start(step):
         for i in range(2):
@@ -364,18 +395,25 @@
             for half, part in ((0, 1), (1, 0), (1, 1)):
                 found += dot(own_split[half, at], into_scores[half, part])
             partial[step, at] = found
-        for offset in range(1, side):
-            score_copy(step, 0, offset).start()
+        score_send_all(step, 0)
 
     def score_step(step, phase):
-        for offset in range(1, side):
-            score_copy(step, phase - 1, offset).wait_recv()
-        if phase == 1:
-            over_x[step] = partial[step, x_rows] + from_x[step, 0] + from_x[step, 1] + from_x[step, 2]
-        if phase == 2:
-            over_y[step, y_rows] = over_x[step, y_rows] + from_y[step, 0] + from_y[step, 1] + from_y[step, 2]
-        if phase == 3:
-            scores[step, x_rows] = over_y[step]
+        for group in range(2):
+            for offset in range(1, side):
+                score_copy(step, group, phase - 1, offset).wait_recv()
+            mine = strip(places[1 - group])
+            if phase == 1:
+                found = partial[step, stripe(group, places[group])]
+                for other in range(side - 1):
+                    found += from_along[step, group, other]
+                over_along[step, group] = found
+            if phase == 2:
+                found = over_along[step, group, mine]
+                for other in range(side - 1):
+                    found += from_across[step, group, other]
+                over_both[step, group, mine] = found
+            if phase == 3:
+                scores[step, stripe(group, places[group])] = over_both[step, group]
         if phase == 4:
             for i in range(2):
                 at = slice(i * half_rows, (i + 1) * half_rows)
@@ -385,8 +423,7 @@
                     found += dot(low, from_scores[half], ((1,), (1,)))
                     projected[half, at] = found[:, :LANES] + found[:, LANES:]
             return
-        for offset in range(1, side):
-            score_copy(step, phase, offset).start()
+        score_send_all(step, phase)
 
     loading[0].wait()
     loading[1].wait()
@@ -427,16 +464,15 @@
             loading[9].wait()
 
     def step_body(step, carry):
-        @pl.when(step > 0)
-        def _():
-            score_step(step - 1, 4)
-
         for half in range(2):
             @pl.when(step > 0)
             def _():
                 if half == 1:
                     upper_parts(step - 1, half, 1)
-                finish(step - 1, half)
+                finish_ahead(step - 1, half)
+                if half == 0:
+                    score_step(step - 1, 4)
+                finish_chain(step - 1, half)
 
             @pl.when(step == STEPS)
             def _():
@@ -458,30 +494,30 @@
 
         @pl.when(step < STEPS)
         def _():
+            set_up_factors(step)
+            score_start(step)
             arrive_ahead(step, 0, 0)
             set_up_far(step)
             pass_on(step, 0, 0)
             arrive_chain(step, 0, 0)
             arrive_ahead(step, 1, 0)
             pass_on(step, 1, 0)
-            set_up_factors(step)
-            score_start(step)
             arrive_chain(step, 1, 0)
+            score_step(step, 1)
             set_up(step, 1, 3)
             arrive_ahead(step, 0, 1)
             pass_on(step, 0, 1)
             arrive_chain(step, 0, 1)
-            score_step(step, 1)
+            score_step(step, 2)
             arrive_ahead(step, 1, 1)
             pass_on(step, 1, 1)
             set_up(step, 0, 1)
             diagonal(0)
             arrive_chain(step, 1, 1)
-            score_step(step, 2)
+            score_step(step, 3)
             diagonal(1)
             upper_parts(step, 0, 0)
             upper_parts(step, 1, 0)
-            score_step(step, 3)
             upper_parts(step, 0, 1)
 
         return carry
@@ -506,8 +542,9 @@
     lax.fori_loop(0, 2 * STEPS, drain, 0)
     for step in range(STEPS):
         for phase in range(4):
-            for offset in range(1, side):
-                score_copy(step, phase, offset).wait_send()
+            for group in range(2):
+                for offset in range(1, side):
+                    score_copy(step, group, phase, offset).wait_send()
     for half in range(2):
         write(half).wait()
 
@@ -519,7 +556,7 @@
     blocks = 2 * hops + 1
     f32, bf16 = jnp.float32, jnp.bfloat16
     piece = (rows, LANES)
-    quarter = rows // side
+    quarter = rows // (2 * side)
     dma = pltpu.SemaphoreType.DMA
     scratch = [
         pltpu.VMEM((1,) + ld_width.shape, jnp.int32),
@@ -545,16 +582,16 @@
         pltpu.VMEM((2, 2, 2 * LANES, factors), bf16),
         pltpu.VMEM((2, 2 * LANES, factors), bf16),
         pltpu.VMEM((STEPS, rows, factors), f32),
-        pltpu.VMEM((STEPS, side - 1, quarter, factors), f32),
-        pltpu.VMEM((STEPS, quarter, factors), f32),
-        pltpu.VMEM((STEPS, side - 1, quarter // side, factors), f32),
-        pltpu.VMEM((STEPS, quarter, factors), f32),
+        pltpu.VMEM((STEPS, 2, side - 1, quarter, factors), f32),
+        pltpu.VMEM((STEPS, 2, quarter, factors), f32),
+        pltpu.VMEM((STEPS, 2, side - 1, quarter // side, factors), f32),
+        pltpu.VMEM((STEPS, 2, quarter, factors), f32),
         pltpu.VMEM((STEPS, rows, factors), f32),
         pltpu.VMEM((2,) + piece, f32),
         dma((10,)),
     ]
     scratch += [dma((STEPS, 2, hops)) for _ in range(8)]
-    scratch += [dma((STEPS, 4, side - 1)) for _ in range(2)]
+    scratch += [dma((STEPS, 2, 4, side - 1)) for _ in range(2)]
 
     def call(*refs):
         kernel(total_rows, side, *refs)

time: 98.7 us -> 86.8 us (0.88)
  Pallas kernels: 96.7 us -> 84.8 us
    pallas_call x1, Pallas kernels: 96.7 us -> 84.8 us  [body(): pl.pallas_call(call, name='fit', out_shape=jax.ShapeDtypeStruct(effects_i...]
where the time goes in v4:
time: 86.8 us; the launch traced here: 86.7 us
  Pallas kernels  84.8 us (98%)
  local copies, waits for them, and re-layouts  1.87 us (2%)
    pallas_call x1, Pallas kernels, body(): pl.pallas_call(call, name='fit', out_shape=jax.ShapeDtypeStruct(effects_i...  84.8 us
    unnamed x1, local copies, waits for them, and re-layouts  1.87 us

profile of v4, /device:TPU:1, one launch (start us, length us, event | category | flops | bytes accessed | tf_op | source)
XLA Modules:
  0.0 86.7 jit_solution(13631322953128920158)
XLA Ops:
  0.0 84.8 %fit.1 = f32[512,256]{1,0:T(8,128)} custom-call(f32[512,3072]{1,0:T(8,128)} %refs_0_.1, f32[512,256]{1,0:T(8,128)} %refs_1_.1, f32[512,256]{1,0:T(8,128)} %refs_2_.1, f32[256,256]{1,0:T(8,128)} %refs_3_.1, f32[256,256]{1,0:T(8,128)} %refs_4_.1, s32[1,64]{1,0:T(1,128)} %bitcast.2, s32[1,64]{1,0:T(1,128)} %bitcast.3), custom_call_target="tpu_custom_call" | custom-call | tf_op jit(solution)/shard_map/fit/pallas_call | solution.py:600
  84.8 1.9 %copy.9 = f32[512,256]{1,0:T(8,128)} copy(f32[512,256]{1,0:T(8,128)} %fit.1) | data formatting | bytes 1048576

commit v5 on v4

--- a/solution.py
+++ b/solution.py
@@ -84,6 +84,8 @@
     column = lax.axis_index("trait")
     devices = lax.axis_size("snp")
     core = lax.rem(device, 2)
+    chip = lax.div(device, 2)
+    chips = devices // 2
     behind_id = (lax.rem(device + devices - 2, devices), column)
     ahead_id = (lax.rem(device + 2, devices), column)
     beside_id = (device + 1 - 2 * core, column)
@@ -119,13 +121,23 @@
     for copy in loading:
         copy.start()
 
-    partners = [behind_id, ahead_id, beside_id]
+    partners = [beside_id]
     for offset in range(1, side):
         partners += [x_id(offset), y_id(offset)]
     barrier = pltpu.get_barrier_semaphore()
     for partner in partners:
         pl.semaphore_signal(barrier, inc=1, device_id=partner, device_id_type=MESH)
-    pl.semaphore_wait(barrier, len(partners))
+
+    @pl.when(chip >= 1)
+    def _():
+        pl.semaphore_signal(barrier, inc=1, device_id=behind_id, device_id_type=MESH)
+
+    @pl.when(chip + 1 < chips)
+    def _():
+        pl.semaphore_signal(barrier, inc=1, device_id=ahead_id, device_id_type=MESH)
+
+    ends = jnp.where(chip >= 1, 1, 0) + jnp.where(chip + 1 < chips, 1, 0)
+    pl.semaphore_wait(barrier, len(partners) + ends)
 
     def remote(source, target, send, recv, to):
         return pltpu.make_async_remote_copy(
@@ -171,8 +183,28 @@
             beside_id,
         )
 
+    def sends_ahead(slot):
+        return (chip >= 1) & (chip + slot < chips)
+
+    def takes_ahead(slot):
+        return chip + 1 + slot < chips
+
+    def takes_beside(slot):
+        return chip + slot + core < chips
+
+    def sends_beside(slot):
+        return chip + 1 - core + slot < chips
+
+    def sends_chain(slot):
+        return chip + hops - slot < chips
+
+    def takes_chain(slot):
+        return (chip >= 1) & (chip + hops - 1 - slot < chips)
+
     def send_own(step, half):
-        ahead_copy(step, half, 0).start()
+        @pl.when(sends_ahead(0))
+        def _():
+            ahead_copy(step, half, 0).start()
 
         @pl.when(core == 1)
         def _():
@@ -180,7 +212,10 @@
 
     for half in range(2):
         source = effects_hbm.at[:, pl.ds(half * LANES, LANES)]
-        ahead_copy(0, half, 0, source).start()
+
+        @pl.when(sends_ahead(0))
+        def _():
+            ahead_copy(0, half, 0, source).start()
 
         @pl.when(core == 1)
         def _():
@@ -284,45 +319,80 @@
             cross_copy(step, half, 0).wait_recv()
             first[step, half] += crossed[step, half, 0]
 
-        chain_copy(step, half, 0).start()
+        @pl.when(sends_chain(0))
+        def _():
+            chain_copy(step, half, 0).start()
+
+    def ahead_part(step, half, slot):
+        @pl.when(takes_ahead(slot))
+        def _():
+            product(2 * slot + 2, joined(ahead[step, half, slot]), add_to(total.at[half]))
+
+    def beside_part(step, half, slot):
+        @pl.when(takes_beside(slot))
+        def _():
+            beside_copy(own.at[step, half], step, half, slot).wait_recv()
+            product(2 * slot + 1, joined(beside[step, half, slot]), add_to(total.at[half]))
 
     def finish_ahead(step, half):
         last = hops - 1
-        ahead_copy(step, half, last).wait_recv()
-
-        @pl.when(core == 0)
-        def _():
-            beside_copy(ahead.at[step, half, last], step, half, last).start()
-
-        product(2 * hops, joined(ahead[step, half, last]), add_to(total.at[half]))
+
+        @pl.when(takes_ahead(last))
+        def _():
+            ahead_copy(step, half, last).wait_recv()
+
+            @pl.when(core == 0)
+            def _():
+                beside_copy(ahead.at[step, half, last], step, half, last).start()
+
+        ahead_part(step, half, last)
 
         @pl.when(core == 1)
         def _():
             cross_copy(step, half, last).wait_recv()
             home[half] += crossed[step, half, last]
 
-        beside_copy(own.at[step, half], step, half, last).wait_recv()
-        product(2 * hops - 1, joined(beside[step, half, last]), add_to(total.at[half]))
+        beside_part(step, half, last)
+        total[half] += home[half]
 
     def finish_chain(step, half):
         last = hops - 1
-        chain_copy(step, half, last).wait_recv()
+
+        @pl.when(takes_chain(last))
+        def _():
+            chain_copy(step, half, last).wait_recv()
+            total[half] += chain[step, half, last]
+
         effects = own[step, half]
-        product_sum = total[half] + (home[half] + chain[step, half, last])
-        gradient = effects + product_sum - marginal[half] + shrinkage * (effects - projected[half])
+        gradient = effects + total[half] - marginal[half] + shrinkage * (effects - projected[half])
         own[step + 1, half] = effects - step_size * gradient
 
     def arrive_ahead(step, half, slot):
-        ahead_copy(step, half, slot).wait_recv()
-        ahead_copy(step, half, slot + 1).start()
-        beside_copy(ahead.at[step, half, slot], step, half, slot + core).start()
+        @pl.when(takes_ahead(slot))
+        def _():
+            ahead_copy(step, half, slot).wait_recv()
+            beside_copy(ahead.at[step, half, slot], step, half, slot + core).start()
+
+        @pl.when(sends_ahead(slot + 1))
+        def _():
+            ahead_copy(step, half, slot + 1).start()
 
     def arrive_chain(step, half, slot):
         cross_copy(step, half, slot + 1 - core).wait_recv()
         later[half] += crossed[step, half, slot + 1 - core]
-        chain_copy(step, half, slot).wait_recv()
-        chain[step, half, slot] += later[half]
-        chain_copy(step, half, slot + 1).start()
+
+        @pl.when(takes_chain(slot))
+        def _():
+            chain_copy(step, half, slot).wait_recv()
+            chain[step, half, slot] += later[half]
+
+        @pl.when(chip == 0)
+        def _():
+            chain[step, half, slot] = later[half]
+
+        @pl.when(sends_chain(slot + 1))
+        def _():
+            chain_copy(step, half, slot + 1).start()
 
     def pass_on(step, half, slot):
         block = 2 * (hops - 1 - slot)
@@ -335,9 +405,8 @@
         product(0, own_split[half], store_to(total.at[half]))
 
     def upper_parts(step, half, slot):
-        product(2 * slot + 2, joined(ahead[step, half, slot]), add_to(total.at[half]))
-        beside_copy(own.at[step, half], step, half, slot).wait_recv()
-        product(2 * slot + 1, joined(beside[step, half, slot]), add_to(total.at[half]))
+        ahead_part(step, half, slot)
+        beside_part(step, half, slot)
 
     quarter = half_rows // side
     piece = quarter // side
@@ -533,10 +602,19 @@
         step = lax.div(index, 2)
         half = lax.rem(index, 2)
         for slot in range(hops):
-            ahead_copy(step, half, slot).wait_send()
-            chain_copy(step, half, slot).wait_send()
             cross_copy(step, half, slot).wait_send()
-            beside_copy(own.at[step, half], step, half, slot).wait_send()
+
+            @pl.when(sends_ahead(slot))
+            def _():
+                ahead_copy(step, half, slot).wait_send()
+
+            @pl.when(sends_chain(slot))
+            def _():
+                chain_copy(step, half, slot).wait_send()
+
+            @pl.when(sends_beside(slot))
+            def _():
+                beside_copy(own.at[step, half], step, half, slot).wait_send()
         return carry
 
     lax.fori_loop(0, 2 * STEPS, drain, 0)

time: 86.8 us -> 84.2 us (0.970)
  Pallas kernels: 84.8 us -> 81.8 us
    pallas_call x1, Pallas kernels: 84.8 us -> 81.8 us  [body(): pl.pallas_call(call, name='fit', out_shape=jax.ShapeDtypeStruct(effects_i...]
where the time goes in v5:
time: 84.2 us; the launch traced here: 83.7 us
  Pallas kernels  81.8 us (97%)
  local copies, waits for them, and re-layouts  1.87 us (2%)
    pallas_call x1, Pallas kernels, body(): pl.pallas_call(call, name='fit', out_shape=jax.ShapeDtypeStruct(effects_i...  81.8 us
    unnamed x1, local copies, waits for them, and re-layouts  1.87 us

profile of v5, /device:TPU:1, one launch (start us, length us, event | category | flops | bytes accessed | tf_op | source)
XLA Modules:
  0.0 83.7 jit_solution(7207395584067812526)
XLA Ops:
  0.0 81.8 %fit.1 = f32[512,256]{1,0:T(8,128)} custom-call(f32[512,3072]{1,0:T(8,128)} %refs_0_.1, f32[512,256]{1,0:T(8,128)} %refs_1_.1, f32[512,256]{1,0:T(8,128)} %refs_2_.1, f32[256,256]{1,0:T(8,128)} %refs_3_.1, f32[256,256]{1,0:T(8,128)} %refs_4_.1, s32[1,64]{1,0:T(1,128)} %bitcast.2, s32[1,64]{1,0:T(1,128)} %bitcast.3), custom_call_target="tpu_custom_call" | custom-call | tf_op jit(solution)/shard_map/fit/pallas_call | solution.py:678
  81.8 1.9 %copy.9 = f32[512,256]{1,0:T(8,128)} copy(f32[512,256]{1,0:T(8,128)} %fit.1) | data formatting | bytes 1048576

commit v6 on v5

--- a/solution.py
+++ b/solution.py
@@ -39,6 +39,8 @@
     starts,
     band,
     reach,
+    stacked,
+    rotated,
     upper,
     own,
     own_split,
@@ -104,6 +106,21 @@
     def y_id(offset):
         return (device, y_peer(offset) * side + my_x)
 
+    partners = [beside_id]
+    for offset in range(1, side):
+        partners += [x_id(offset), y_id(offset)]
+    barrier = pltpu.get_barrier_semaphore()
+    for partner in partners:
+        pl.semaphore_signal(barrier, inc=1, device_id=partner, device_id_type=MESH)
+
+    @pl.when(chip >= 1)
+    def _():
+        pl.semaphore_signal(barrier, inc=1, device_id=behind_id, device_id_type=MESH)
+
+    @pl.when(chip + 1 < chips)
+    def _():
+        pl.semaphore_signal(barrier, inc=1, device_id=ahead_id, device_id_type=MESH)
+
     near = 2 * rows * (hops - 1)
     loads = [
         (width_hbm, width),
@@ -118,23 +135,8 @@
         (marginal_hbm.at[:, pl.ds(LANES, LANES)], marginal.at[1]),
     ]
     loading = [pltpu.make_async_copy(a, b, load_sem.at[i]) for i, (a, b) in enumerate(loads)]
-    for copy in loading:
-        copy.start()
-
-    partners = [beside_id]
-    for offset in range(1, side):
-        partners += [x_id(offset), y_id(offset)]
-    barrier = pltpu.get_barrier_semaphore()
-    for partner in partners:
-        pl.semaphore_signal(barrier, inc=1, device_id=partner, device_id_type=MESH)
-
-    @pl.when(chip >= 1)
-    def _():
-        pl.semaphore_signal(barrier, inc=1, device_id=behind_id, device_id_type=MESH)
-
-    @pl.when(chip + 1 < chips)
-    def _():
-        pl.semaphore_signal(barrier, inc=1, device_id=ahead_id, device_id_type=MESH)
+    for index in (4, 0, 1, 2, 3, 5, 6, 7, 8, 9):
+        loading[index].start()
 
     ends = jnp.where(chip >= 1, 1, 0) + jnp.where(chip + 1 < chips, 1, 0)
     pl.semaphore_wait(barrier, len(partners) + ends)
@@ -234,34 +236,45 @@
     half_rows = rows // 2
     per_block = rows // LANES
 
+    def turn(chunk):
+        def spread(group, carry):
+            for part in range(2):
+                at = pl.multiple_of(group * GROUP + part * 8, 8)
+                for tile in range(8):
+                    lanes = slice((chunk * 8 + tile) * LANES, (chunk * 8 + tile + 1) * LANES)
+                    stacked[pl.ds((chunk * rows + at) * 8 + tile, 8, stride=8), :] = band[pl.ds(at, 8), lanes]
+            return carry
+
+        def rotate(group, carry):
+            for row in range(LANES):
+                at = pl.multiple_of((chunk * rows + group * LANES + row) * 8, 8)
+                values = stacked[pl.ds(at, 8), :]
+                rotated[pl.ds(at, 8), :] = values if row + 1 == LANES else pltpu.roll(values, row + 1, 1)
+            return carry
+
+        lax.fori_loop(0, rows // GROUP, spread, 0)
+        lax.fori_loop(0, rows // LANES, rotate, 0)
+
     def shear(low_block, high_block):
         def body(group, carry):
             shift = group * GROUP
             lane = lax.broadcasted_iota(jnp.int32, (GROUP, LANES), 1)
             row = lax.broadcasted_iota(jnp.int32, (GROUP, LANES), 0)
-            row8 = lax.broadcasted_iota(jnp.int32, (8, LANES), 0)
             from_left = lane < row + (shift + 1)
             for base in range(rows // LANES):
                 at = pl.multiple_of(base * LANES + shift, GROUP)
-                limit = reach[pl.ds(at, GROUP), :]
+                limit = reach[pl.ds(at, GROUP), :] + (row - lane) + (at + 1)
 
                 def turned(tile):
                     if tile < 0 or tile >= span // LANES:
                         return jnp.zeros((GROUP, LANES), jnp.float32)
-                    values = band[pl.ds(at, GROUP), tile * LANES : (tile + 1) * LANES]
-                    values = jnp.where(lane + tile * LANES < limit, values, 0.0)
-                    parts = []
-                    for top in range(0, GROUP, 8):
-                        part = pltpu.roll(values[top : top + 8], shift + (top + 1), 1)
-                        for bit in (1, 2, 4):
-                            part = jnp.where(row8 & bit != 0, pltpu.roll(part, bit, 1), part)
-                        parts.append(part)
-                    return jnp.concatenate(parts, axis=0)
+                    return rotated[pl.ds((tile // 8 * rows + at) * 8 + tile % 8, GROUP, stride=8), :]
 
                 left = turned(low_block * per_block - base - 1)
                 for tile in range(low_block * per_block, high_block * per_block):
                     right = turned(tile - base)
-                    high, low = split(jnp.where(from_left, left, right))
+                    values = jnp.where(from_left, left, right)
+                    high, low = split(jnp.where(tile * LANES < limit, values, 0.0))
                     left = right
                     block, at_tile = tile // per_block, tile % per_block
                     row_half = base * LANES // half_rows
@@ -310,8 +323,14 @@
                 own_stack[half, at : at + half_rows] = found[i * half_rows : (i + 1) * half_rows]
 
     def start(step, half):
-        lower_part(2 * hops - 1, half, crossing.at[step, half, 0])
-        cross_copy(step, half, 0).start()
+        def send_beside():
+            lower_part(2 * hops - 1, half, crossing.at[step, half, 0])
+            cross_copy(step, half, 0).start()
+
+        @pl.when(core == 1)
+        def _():
+            send_beside()
+
         lower_part(2 * hops, half, first.at[step, half])
 
         @pl.when(core == 0)
@@ -322,6 +341,10 @@
         @pl.when(sends_chain(0))
         def _():
             chain_copy(step, half, 0).start()
+
+        @pl.when(core == 0)
+        def _():
+            send_beside()
 
     def ahead_part(step, half, slot):
         @pl.when(takes_ahead(slot))
@@ -501,20 +524,21 @@
     loading[3].wait()
     take_own(0, 0)
     loading[4].wait()
+    turn(2)
     shear(2 * hops - 1, 2 * hops + 1)
 
     def set_up(step, low, high):
         @pl.when(step == 0)
         def _():
-            for block in range(high - 1, low - 1, -1):
-                shear(block, block + 1)
+            shear(low, high)
 
     def set_up_far(step):
         @pl.when(step == 0)
         def _():
             loading[5].wait()
-            shear(2 * hops - 2, 2 * hops - 1)
-            shear(2 * hops - 3, 2 * hops - 2)
+            turn(1)
+            shear(2 * hops - 3, 2 * hops - 1)
+            turn(0)
 
     def set_up_factors(step):
         @pl.when(step == 0)
@@ -641,6 +665,8 @@
         pltpu.VMEM((1,) + ld_starts.shape, jnp.int32),
         pltpu.VMEM((rows, span), f32),
         pltpu.VMEM((rows, LANES), jnp.int32),
+        pltpu.VMEM((rows * span // LANES, LANES), f32),
+        pltpu.VMEM((rows * span // LANES, LANES), f32),
         pltpu.VMEM((blocks, 2, 2, rows // 2, rows), bf16),
         pltpu.VMEM((STEPS + 1, 2) + piece, f32),
         pltpu.VMEM((2, rows, 2 * LANES), bf16),

time: 84.2 us -> 82.1 us (0.975)
  Pallas kernels: 81.8 us -> 79.7 us
    pallas_call x1, Pallas kernels: 81.8 us -> 79.7 us  [body(): pl.pallas_call(call, name='fit', out_shape=jax.ShapeDtypeStruct(effects_i...]
where the time goes in v6:
time: 82.1 us; the launch traced here: 81.6 us
  Pallas kernels  79.7 us (97%)
  local copies, waits for them, and re-layouts  1.87 us (2%)
    pallas_call x1, Pallas kernels, body(): pl.pallas_call(call, name='fit', out_shape=jax.ShapeDtypeStruct(effects_i...  79.7 us
    unnamed x1, local copies, waits for them, and re-layouts  1.87 us

profile of v6, /device:TPU:1, one launch (start us, length us, event | category | flops | bytes accessed | tf_op | source)
XLA Modules:
  0.0 81.6 jit_solution(18435888115736709413)
XLA Ops:
  0.0 79.7 %fit.1 = f32[512,256]{1,0:T(8,128)} custom-call(f32[512,3072]{1,0:T(8,128)} %refs_0_.1, f32[512,256]{1,0:T(8,128)} %refs_1_.1, f32[512,256]{1,0:T(8,128)} %refs_2_.1, f32[256,256]{1,0:T(8,128)} %refs_3_.1, f32[256,256]{1,0:T(8,128)} %refs_4_.1, s32[1,64]{1,0:T(1,128)} %bitcast.2, s32[1,64]{1,0:T(1,128)} %bitcast.3), custom_call_target="tpu_custom_call" | custom-call | tf_op jit(solution)/shard_map/fit/pallas_call | solution.py:704
  79.7 1.9 %copy.9 = f32[512,256]{1,0:T(8,128)} copy(f32[512,256]{1,0:T(8,128)} %fit.1) | data formatting | bytes 1048576

commit v7 on v6

--- a/solution.py
+++ b/solution.py
@@ -127,15 +127,17 @@
         (starts_hbm, starts),
         (effects_hbm.at[:, pl.ds(0, LANES)], own.at[0, 0]),
         (effects_hbm.at[:, pl.ds(LANES, LANES)], own.at[0, 1]),
-        (band_hbm.at[:, pl.ds(near, span - near)], band.at[:, pl.ds(near, span - near)]),
         (band_hbm.at[:, pl.ds(0, near)], band.at[:, pl.ds(0, near)]),
         (factor_in_hbm, factor_in),
         (factor_out_hbm, factor_out),
         (marginal_hbm.at[:, pl.ds(0, LANES)], marginal.at[0]),
         (marginal_hbm.at[:, pl.ds(LANES, LANES)], marginal.at[1]),
     ]
+    for top in range(0, rows, LANES):
+        part = (pl.ds(top, LANES), pl.ds(near, span - near))
+        loads.append((band_hbm.at[part], band.at[part]))
     loading = [pltpu.make_async_copy(a, b, load_sem.at[i]) for i, (a, b) in enumerate(loads)]
-    for index in (4, 0, 1, 2, 3, 5, 6, 7, 8, 9):
+    for index in (0, 1, 9, 10, 11, 12, 2, 3):
         loading[index].start()
 
     ends = jnp.where(chip >= 1, 1, 0) + jnp.where(chip + 1 < chips, 1, 0)
@@ -236,7 +238,7 @@
     half_rows = rows // 2
     per_block = rows // LANES
 
-    def turn(chunk):
+    def turn(chunk, low=0, high=rows // LANES):
         def spread(group, carry):
             for part in range(2):
                 at = pl.multiple_of(group * GROUP + part * 8, 8)
@@ -252,8 +254,8 @@
                 rotated[pl.ds(at, 8), :] = values if row + 1 == LANES else pltpu.roll(values, row + 1, 1)
             return carry
 
-        lax.fori_loop(0, rows // GROUP, spread, 0)
-        lax.fori_loop(0, rows // LANES, rotate, 0)
+        lax.fori_loop(low * (LANES // GROUP), high * (LANES // GROUP), spread, 0)
+        lax.fori_loop(low, high, rotate, 0)
 
     def shear(low_block, high_block):
         def body(group, carry):
@@ -386,9 +388,26 @@
             chain_copy(step, half, last).wait_recv()
             total[half] += chain[step, half, last]
 
-        effects = own[step, half]
-        gradient = effects + total[half] - marginal[half] + shrinkage * (effects - projected[half])
-        own[step + 1, half] = effects - step_size * gradient
+        for i in range(2):
+            at = slice(i * half_rows, (i + 1) * half_rows)
+            effects = own[step, half, at]
+            gradient = (
+                effects
+                + total[half, at]
+                - marginal[half, at]
+                + shrinkage * (effects - projected[half, at])
+            )
+            own[step + 1, half, at] = effects - step_size * gradient
+
+            @pl.when(step + 1 == STEPS)
+            def _():
+                write(half, i).start()
+
+    def write(half, i):
+        at = pl.ds(i * half_rows, half_rows)
+        return pltpu.make_async_copy(
+            own.at[STEPS, half, at], out_hbm.at[at, pl.ds(half * LANES, LANES)], load_sem.at[2 * half + i]
+        )
 
     def arrive_ahead(step, half, slot):
         @pl.when(takes_ahead(slot))
@@ -517,14 +536,42 @@
             return
         score_send_all(step, phase)
 
+    def drain(step, half, slot):
+        cross_copy(step, half, slot).wait_send()
+
+        @pl.when(sends_ahead(slot))
+        def _():
+            ahead_copy(step, half, slot).wait_send()
+
+        @pl.when(sends_chain(slot))
+        def _():
+            chain_copy(step, half, slot).wait_send()
+
+        @pl.when(sends_beside(slot))
+        def _():
+            beside_copy(own.at[step, half], step, half, slot).wait_send()
+
+    def drain_step(step):
+        for half in range(2):
+            for slot in range(hops):
+                if half == 0 or slot < hops - 1:
+                    drain(step, half, slot)
+        for phase in range(4):
+            for group in range(2):
+                for offset in range(1, side):
+                    score_copy(step, group, phase, offset).wait_send()
+
     loading[0].wait()
     loading[1].wait()
     find_reach()
+    for part in range(rows // LANES):
+        loading[9 + part].wait()
+        turn(2, part, part + 1)
+    for index in range(4, 9):
+        loading[index].start()
     loading[2].wait()
     loading[3].wait()
     take_own(0, 0)
-    loading[4].wait()
-    turn(2)
     shear(2 * hops - 1, 2 * hops + 1)
 
     def set_up(step, low, high):
@@ -535,7 +582,7 @@
     def set_up_far(step):
         @pl.when(step == 0)
         def _():
-            loading[5].wait()
+            loading[4].wait()
             turn(1)
             shear(2 * hops - 3, 2 * hops - 1)
             turn(0)
@@ -543,8 +590,8 @@
     def set_up_factors(step):
         @pl.when(step == 0)
         def _():
+            loading[5].wait()
             loading[6].wait()
-            loading[7].wait()
             for half in range(2):
                 at = slice(half * LANES, (half + 1) * LANES)
                 for part, values in enumerate(split(factor_in[at, :])):
@@ -553,8 +600,8 @@
                 high, low = split(factor_out[at, :])
                 from_scores[half, :LANES] = high
                 from_scores[half, LANES:] = low
+            loading[7].wait()
             loading[8].wait()
-            loading[9].wait()
 
     def step_body(step, carry):
         for half in range(2):
@@ -565,11 +612,13 @@
                 finish_ahead(step - 1, half)
                 if half == 0:
                     score_step(step - 1, 4)
+                else:
+
+                    @pl.when(step == STEPS)
+                    def _():
+                        drain_step(step - 1)
+
                 finish_chain(step - 1, half)
-
-            @pl.when(step == STEPS)
-            def _():
-                write(half).start()
 
             @pl.when(step == 1)
             def _():
@@ -608,6 +657,12 @@
             diagonal(0)
             arrive_chain(step, 1, 1)
             score_step(step, 3)
+
+            @pl.when(step > 0)
+            def _():
+                drain_step(step - 1)
+                drain(step - 1, 1, hops - 1)
+
             diagonal(1)
             upper_parts(step, 0, 0)
             upper_parts(step, 1, 0)
@@ -615,40 +670,12 @@
 
         return carry
 
-    def write(half):
-        return pltpu.make_async_copy(
-            own.at[STEPS, half], out_hbm.at[:, pl.ds(half * LANES, LANES)], load_sem.at[half]
-        )
-
     lax.fori_loop(0, STEPS + 1, step_body, 0)
 
-    def drain(index, carry):
-        step = lax.div(index, 2)
-        half = lax.rem(index, 2)
-        for slot in range(hops):
-            cross_copy(step, half, slot).wait_send()
-
-            @pl.when(sends_ahead(slot))
-            def _():
-                ahead_copy(step, half, slot).wait_send()
-
-            @pl.when(sends_chain(slot))
-            def _():
-                chain_copy(step, half, slot).wait_send()
-
-            @pl.when(sends_beside(slot))
-            def _():
-                beside_copy(own.at[step, half], step, half, slot).wait_send()
-        return carry
-
-    lax.fori_loop(0, 2 * STEPS, drain, 0)
-    for step in range(STEPS):
-        for phase in range(4):
-            for group in range(2):
-                for offset in range(1, side):
-                    score_copy(step, group, phase, offset).wait_send()
+    drain(STEPS - 1, 1, hops - 1)
     for half in range(2):
-        write(half).wait()
+        for i in range(2):
+            write(half, i).wait()
 
 
 def body(total_rows, side, ld_band, marginal, effects_init, factor_in, factor_out, ld_width, ld_starts):
@@ -692,7 +719,7 @@
         pltpu.VMEM((STEPS, 2, quarter, factors), f32),
         pltpu.VMEM((STEPS, rows, factors), f32),
         pltpu.VMEM((2,) + piece, f32),
-        dma((10,)),
+        dma((9 + rows // LANES,)),
     ]
     scratch += [dma((STEPS, 2, hops)) for _ in range(8)]
     scratch += [dma((STEPS, 2, 4, side - 1)) for _ in range(2)]

time: 82.1 us -> 82.2 us (level)
  no operation moved by 1% of the time
where the time goes in v7:
time: 82.2 us; the launch traced here: 81.7 us
  Pallas kernels  79.8 us (97%)
  local copies, waits for them, and re-layouts  1.87 us (2%)
    pallas_call x1, Pallas kernels, body(): pl.pallas_call(call, name='fit', out_shape=jax.ShapeDtypeStruct(effects_i...  79.8 us
    unnamed x1, local copies, waits for them, and re-layouts  1.87 us

profile of v7, /device:TPU:1, one launch (start us, length us, event | category | flops | bytes accessed | tf_op | source)
XLA Modules:
  0.0 81.7 jit_solution(9009011994388178166)
XLA Ops:
  0.0 79.8 %fit.1 = f32[512,256]{1,0:T(8,128)} custom-call(f32[512,3072]{1,0:T(8,128)} %refs_0_.1, f32[512,256]{1,0:T(8,128)} %refs_1_.1, f32[512,256]{1,0:T(8,128)} %refs_2_.1, f32[256,256]{1,0:T(8,128)} %refs_3_.1, f32[256,256]{1,0:T(8,128)} %refs_4_.1, s32[1,64]{1,0:T(1,128)} %bitcast.2, s32[1,64]{1,0:T(1,128)} %bitcast.3), custom_call_target="tpu_custom_call" | custom-call | tf_op jit(solution)/shard_map/fit/pallas_call | solution.py:731
  79.8 1.9 %copy.9 = f32[512,256]{1,0:T(8,128)} copy(f32[512,256]{1,0:T(8,128)} %fit.1) | data formatting | bytes 1048576

commit v8 on v7

--- a/solution.py
+++ b/solution.py
@@ -141,7 +141,6 @@
         loading[index].start()
 
     ends = jnp.where(chip >= 1, 1, 0) + jnp.where(chip + 1 < chips, 1, 0)
-    pl.semaphore_wait(barrier, len(partners) + ends)
 
     def remote(source, target, send, recv, to):
         return pltpu.make_async_remote_copy(
@@ -214,16 +213,26 @@
         def _():
             beside_copy(own.at[step, half], step, half, 0).start()
 
-    for half in range(2):
-        source = effects_hbm.at[:, pl.ds(half * LANES, LANES)]
-
-        @pl.when(sends_ahead(0))
-        def _():
-            ahead_copy(0, half, 0, source).start()
-
-        @pl.when(core == 1)
-        def _():
-            beside_copy(source, 0, half, 0).start()
+    def enter():
+        pl.semaphore_wait(barrier, len(partners) + ends)
+        for half in range(2):
+            source = effects_hbm.at[:, pl.ds(half * LANES, LANES)]
+            at_first = ahead_copy(0, half, 0, source)
+            to_beside = beside_copy(source, 0, half, 0)
+
+            @pl.when(sends_ahead(0))
+            def _():
+                at_first.start()
+
+            @pl.when(core == 1)
+            def _():
+                to_beside.start()
+
+    early = chip < chips // 2
+
+    @pl.when(jnp.logical_not(early))
+    def _():
+        enter()
 
     def find_reach():
         for base in range(0, rows, LANES):
@@ -573,6 +582,10 @@
     loading[3].wait()
     take_own(0, 0)
     shear(2 * hops - 1, 2 * hops + 1)
+
+    @pl.when(early)
+    def _():
+        enter()
 
     def set_up(step, low, high):
         @pl.when(step == 0)

time: 82.2 us -> 82.2 us (level)
  no operation moved by 1% of the time
where the time goes in v8:
time: 82.2 us; the launch traced here: 81.7 us
  Pallas kernels  79.8 us (97%)
  local copies, waits for them, and re-layouts  1.87 us (2%)
    pallas_call x1, Pallas kernels, body(): pl.pallas_call(call, name='fit', out_shape=jax.ShapeDtypeStruct(effects_i...  79.8 us
    unnamed x1, local copies, waits for them, and re-layouts  1.87 us

profile of v8, /device:TPU:1, one launch (start us, length us, event | category | flops | bytes accessed | tf_op | source)
XLA Modules:
  0.0 81.7 jit_solution(3466786159683069646)
XLA Ops:
  0.0 79.8 %fit.1 = f32[512,256]{1,0:T(8,128)} custom-call(f32[512,3072]{1,0:T(8,128)} %refs_0_.1, f32[512,256]{1,0:T(8,128)} %refs_1_.1, f32[512,256]{1,0:T(8,128)} %refs_2_.1, f32[256,256]{1,0:T(8,128)} %refs_3_.1, f32[256,256]{1,0:T(8,128)} %refs_4_.1, s32[1,64]{1,0:T(1,128)} %bitcast.2, s32[1,64]{1,0:T(1,128)} %bitcast.3), custom_call_target="tpu_custom_call" | custom-call | tf_op jit(solution)/shard_map/fit/pallas_call | solution.py:744
  79.8 1.9 %copy.9 = f32[512,256]{1,0:T(8,128)} copy(f32[512,256]{1,0:T(8,128)} %fit.1) | data formatting | bytes 1048576

commit v9 on v8

--- a/solution.py
+++ b/solution.py
@@ -622,15 +622,14 @@
             def _():
                 if half == 1:
                     upper_parts(step - 1, half, 1)
+
+                    @pl.when(step == STEPS)
+                    def _():
+                        drain_step(step - 1)
+
                 finish_ahead(step - 1, half)
                 if half == 0:
                     score_step(step - 1, 4)
-                else:
-
-                    @pl.when(step == STEPS)
-                    def _():
-                        drain_step(step - 1)
-
                 finish_chain(step - 1, half)
 
             @pl.when(step == 1)

time: 82.2 us -> 82.2 us (level)
  no operation moved by 1% of the time
where the time goes in v9:
time: 82.2 us; the launch traced here: 81.7 us
  Pallas kernels  79.8 us (97%)
  local copies, waits for them, and re-layouts  1.87 us (2%)
    pallas_call x1, Pallas kernels, body(): pl.pallas_call(call, name='fit', out_shape=jax.ShapeDtypeStruct(effects_i...  79.8 us
    unnamed x1, local copies, waits for them, and re-layouts  1.87 us

profile of v9, /device:TPU:1, one launch (start us, length us, event | category | flops | bytes accessed | tf_op | source)
XLA Modules:
  0.0 81.7 jit_solution(14549438072966434481)
XLA Ops:
  0.0 79.8 %fit.1 = f32[512,256]{1,0:T(8,128)} custom-call(f32[512,3072]{1,0:T(8,128)} %refs_0_.1, f32[512,256]{1,0:T(8,128)} %refs_1_.1, f32[512,256]{1,0:T(8,128)} %refs_2_.1, f32[256,256]{1,0:T(8,128)} %refs_3_.1, f32[256,256]{1,0:T(8,128)} %refs_4_.1, s32[1,64]{1,0:T(1,128)} %bitcast.2, s32[1,64]{1,0:T(1,128)} %bitcast.3), custom_call_target="tpu_custom_call" | custom-call | tf_op jit(solution)/shard_map/fit/pallas_call | solution.py:743
  79.8 1.9 %copy.9 = f32[512,256]{1,0:T(8,128)} copy(f32[512,256]{1,0:T(8,128)} %fit.1) | data formatting | bytes 1048576
